TPU v7x, 256 devices: a whole 4x4x8 slice. The times are simulated.
256 devices in a mesh: dom: 64 (over z, x, core), grp: 4 (over y).
Axes of the slice: x: 4, y: 4, z: 8, core: 2. Of those that a mesh axis runs over, the one named last changes fastest.
Arguments:
- blocks: bfloat16 [12288, 6, 128, 128], P(('dom', 'grp')), may hold values from -0.21875 to 0.21875
- local_cols: int32 [12288, 4], P(('dom', 'grp')), may hold values from 0 to 191
- remote_refs: int32 [12288, 2], P(('dom', 'grp')), may hold values from 0 to 191
- send_blocks: int32 [64, 4, 64, 3], P('dom', 'grp'), may hold values from 0 to 47
- send_counts: int32 [64, 4, 64], P('dom', 'grp'), may hold values from 0 to 3
- probes: bfloat16 [64, 1572864], P(None, ('dom', 'grp')), may hold values from -6 to 6
Outputs:
- moments: float32 [3, 1572864], P(None, ('dom', 'grp'))
All inputs are finite; a program needn't handle non-finite values.
Results may differ from a plain program's by a relative error of at most 0.00064.
Values may be sent and summed in bfloat16 or wider, within the bound.
No kernel may reach another device: no remote copies, remote signals or barrier semaphores. Data moves between devices by JAX's collectives and lax.ppermute only.
A program may use at most 64 MiB of HBM per device.

v0:
```python
import math

import jax
import jax.numpy as jnp
from jax import lax
from jax.sharding import PartitionSpec as P

PROBES = 64
LOCAL = 4
KMOM = 256


def jackson(order, total):
    angle = math.pi / (total + 1)
    return (
        (total - order + 1) * math.cos(order * angle) + math.sin(order * angle) / math.tan(angle)
    ) / (total + 1)


def send_boundary(own, send_list, live):
    outgoing = jnp.take(own, send_list, axis=1)
    outgoing = jnp.where(live[None, :, :, None], outgoing, jnp.zeros_like(outgoing))
    received = lax.all_to_all(outgoing, "dom", split_axis=1, concat_axis=1, tiled=True)
    return received.reshape(own.shape[0], -1, own.shape[2])


def on_device(blocks, local_cols, remote_refs, send_blocks, send_counts, probes):
    rows_here = blocks.shape[0]
    size_block = blocks.shape[2]
    probe_count = probes.shape[0]
    local_blocks = blocks[:, :LOCAL]
    remote_blocks = blocks[:, LOCAL:]
    send_list = send_blocks[0, 0]
    slot_index = jnp.arange(send_list.shape[1], dtype=jnp.int32)
    live = slot_index[None, :] < send_counts[0, 0][:, None]

    def local_part(own):
        panel_all = lax.all_gather(own, "grp", axis=1, tiled=True)
        picked = jnp.take(panel_all, local_cols, axis=1)
        return jnp.einsum(
            "rjab,prjb->pra", local_blocks, picked, preferred_element_type=jnp.float32
        )

    def remote_part(received):
        picked = jnp.take(received, remote_refs, axis=1)
        return jnp.einsum(
            "rjab,prjb->pra", remote_blocks, picked, preferred_element_type=jnp.float32
        )

    def apply_op(field):
        own = field.reshape(probe_count, rows_here, size_block)
        local_sum = local_part(own)
        received = send_boundary(own, send_list, live)
        result = local_sum + remote_part(received)
        return result.reshape(probe_count, rows_here * size_block)

    first = apply_op(probes).astype(jnp.bfloat16)
    base = probes.astype(jnp.float32)
    second = 2.0 * apply_op(first) - base
    norm = 1.0 / math.sqrt(PROBES)
    moment_zero = jackson(0, KMOM) * norm * jnp.sum(base * base, axis=0)
    moment_one = 2.0 * jackson(1, KMOM) * norm * jnp.sum(base * first.astype(jnp.float32), axis=0)
    moment_two = 2.0 * jackson(2, KMOM) * norm * jnp.sum(base * second, axis=0)
    return jnp.stack([moment_zero, moment_one, moment_two], axis=0)


def solution(mesh):
    in_specs = (
        P(("dom", "grp"), None, None, None),
        P(("dom", "grp"), None),
        P(("dom", "grp"), None),
        P("dom", "grp", None, None),
        P("dom", "grp", None),
        P(None, ("dom", "grp")),
    )
    out_specs = P(None, ("dom", "grp"))
    return jax.shard_map(
        on_device, mesh=mesh, in_specs=in_specs, out_specs=out_specs, check_vma=False
    )
```

profile of v0, /device:TPU:16, one launch (start us, length us, event | category | flops | bytes accessed | tf_op | source)
XLA Modules:
  0.0 208.0 jit_solution(10266669360849559524)
XLA Ops:
  6.5 0.7 compare_select_fusion
  7.2 0.7 compare_and_fusion.1
  7.9 1.3 copy_bitcast_fusion
  9.4 0.1 reshape.151
  9.5 0.1 copy.51
  9.6 0.7 iota_compare_fusion
  10.4 2.7 %gather_fusion.1 = bf16[192,64,128]{2,1,0:T(8,128)(2,1)} fusion(bf16[64,48,128]{2,0,1:T(8,128)(2,1)S(1)} %copy_bitcast_fusion, s32[1024]{0:T(1024)S(1)} %pad_clamp_fusion.1), kind=kCustom, calls=%fused_computation.1.clone | custom fusion | bytes 6292224 | tf_op jit(solution)/shard_map/jit(_take)/gather | solution.py:21
  13.1 3.3 %bitcast_select_fusion.1 = bf16[64,64,3,128]{3,0,2,1:T(8,128)(2,1)} fusion(bf16[64,3,64,128]{3,2,1,0:T(8,128)(2,1)} %bitcast.78, pred[64,3]{1,0:T(8,128)(4,1)S(1)} %copy.51, pred[64,3]{1,0:T(8,128)(4,1)S(1)} %iota_compare_fusion), kind=kLoop, calls=%fused_computation.12 | loop fusion | flops 3145728 | bytes 6291840 | tf_op jit(solution)/shard_map/jit(_where)/select_n | solution.py:22
  16.5 12.1 %all-to-all-start = ((bf16[64,64,3,128]{3,0,2,1:T(8,128)(2,1)}), bf16[64,64,3,128]{3,0,2,1:T(8,128)(2,1)S(1)}, u32[]{:S(2)}, u32[]{:S(2)}) async-start(bf16[64,64,3,128]{3,0,2,1:T(8,128)(2,1)} %bitcast_select_fusion.1), calls=%async_computation | async-start | bytes 6291456 | tf_op jit(solution)/shard_map/all_to_all | solution.py:23
  28.6 0.7 all-gather.3.cloned.1.call-update
  29.4 0.1 reshape.155
  29.6 0.1 reshape.147
  29.7 0.1 copy.47
  29.9 0.1 copy.50
  30.0 43.3 %all-gather.3.cloned.1.call-done = bf16[64,192,128]{2,0,1:T(8,128)(2,1)} async-done(((bf16[64,48,128]{2,0,1:T(8,128)(2,1)}), bf16[64,192,128]{2,0,1:T(8,128)(2,1)}) %all-gather.3.cloned.1.call-update) | async-done | bytes 3145744 | tf_op jit(solution)/shard_map/all_gather | solution.py:38
  73.3 4.7 %gather_fusion = bf16[192,64,128]{2,1,0:T(8,128)(2,1)} fusion(bf16[64,192,128]{2,0,1:T(8,128)(2,1)} %all-gather.3.cloned.1.call-done, s32[1024]{0:T(1024)S(1)} %pad_clamp_fusion.2), kind=kCustom, calls=%fused_computation.clone | custom fusion | bytes 6292224 | tf_op jit(solution)/shard_map/jit(_take)/gather | solution.py:39
  77.9 7.2 %fusion.2 = f32[48,64,128,1]{2,1,3,0:T(8,128)} fusion(bf16[48,6,128,128]{3,2,1,0:T(8,128)(2,1)} %param.12, bf16[48,4,64,128]{3,2,1,0:T(8,128)(2,1)} %bitcast.83, pred[48,4]{1,0:T(8,128)(4,1)S(1)} %copy.47), kind=kOutput, calls=%fused_computation.8 | convolution fusion | flops 404226048 | bytes 11010240 | tf_op jit(solution)/shard_map/rjab,prjb->pra/dot_general | solution.py:40
  85.2 17.2 %all-to-all-done = bf16[64,64,3,128]{3,0,2,1:T(8,128)(2,1)S(1)} async-done(((bf16[64,64,3,128]{3,0,2,1:T(8,128)(2,1)}), bf16[64,64,3,128]{3,0,2,1:T(8,128)(2,1)S(1)}, u32[]{:S(2)}, u32[]{:S(2)}) %all-to-all-start) | async-done | bytes 3145760 | tf_op jit(solution)/shard_map/all_to_all | solution.py:23
  102.4 1.9 gather_fusion.2
  104.3 4.1 %fusion.36 = bf16[64,48,128]{2,0,1:T(8,128)(2,1)S(1)} fusion(bf16[48,6,128,128]{3,2,1,0:T(8,128)(2,1)} %param.12, bf16[48,2,64,128]{3,2,1,0:T(8,128)(2,1)} %bitcast.84, pred[48,2]{1,0:T(8,128)(4,1)S(1)} %copy.50, f32[48,64,128,1]{2,1,3,0:T(8,128)} %fusion.2), kind=kOutput, calls=%fused_computation.43 | convolution fusion | flops 202899456 | bytes 7077984 | tf_op jit(solution)/shard_map/rjab,prjb->pra/dot_general | solution.py:46
  108.4 2.7 %gather_fusion.4 = bf16[192,64,128]{2,1,0:T(8,128)(2,1)} fusion(bf16[64,48,128]{2,0,1:T(8,128)(2,1)S(1)} %fusion.36, s32[1024]{0:T(1024)S(1)} %pad_clamp_fusion.1), kind=kCustom, calls=%fused_computation.4.clone | custom fusion | bytes 6292224 | tf_op jit(solution)/shard_map/jit(_take)/gather | solution.py:21
  111.2 3.3 %bitcast_select_fusion = bf16[64,64,3,128]{3,0,2,1:T(8,128)(2,1)} fusion(bf16[64,3,64,128]{3,2,1,0:T(8,128)(2,1)} %bitcast.77, pred[64,3]{1,0:T(8,128)(4,1)S(1)} %copy.51, pred[64,3]{1,0:T(8,128)(4,1)S(1)} %iota_compare_fusion), kind=kLoop, calls=%fused_computation.10 | loop fusion | flops 3145728 | bytes 6291840 | tf_op jit(solution)/shard_map/jit(_where)/select_n | solution.py:22
  114.5 5.3 %all-to-all-start.1 = ((bf16[64,64,3,128]{3,0,2,1:T(8,128)(2,1)}), bf16[64,64,3,128]{3,0,2,1:T(8,128)(2,1)S(1)}, u32[]{:S(2)}, u32[]{:S(2)}) async-start(bf16[64,64,3,128]{3,0,2,1:T(8,128)(2,1)} %bitcast_select_fusion), calls=%async_computation.1 | async-start | bytes 6291456 | tf_op jit(solution)/shard_map/all_to_all | solution.py:23
  119.9 0.7 all-gather.5.cloned.1.call-update
  120.6 44.0 %all-gather.5.cloned.1.call-done = bf16[64,192,128]{2,0,1:T(8,128)(2,1)} async-done(((bf16[64,48,128]{2,0,1:T(8,128)(2,1)}), bf16[64,192,128]{2,0,1:T(8,128)(2,1)}) %all-gather.5.cloned.1.call-update) | async-done | bytes 3145744 | tf_op jit(solution)/shard_map/all_gather | solution.py:38
  164.6 4.6 %gather_fusion.3 = bf16[192,64,128]{2,1,0:T(8,128)(2,1)} fusion(bf16[64,192,128]{2,0,1:T(8,128)(2,1)} %all-gather.5.cloned.1.call-done, s32[1024]{0:T(1024)S(1)} %pad_clamp_fusion.2), kind=kCustom, calls=%fused_computation.3.clone | custom fusion | bytes 6292224 | tf_op jit(solution)/shard_map/jit(_take)/gather | solution.py:39
  169.2 7.2 %fusion = f32[48,64,128,1]{2,1,3,0:T(8,128)} fusion(bf16[48,6,128,128]{3,2,1,0:T(8,128)(2,1)} %param.12, bf16[48,4,64,128]{3,2,1,0:T(8,128)(2,1)} %bitcast.82, pred[48,4]{1,0:T(8,128)(4,1)S(1)} %copy.47), kind=kOutput, calls=%fused_computation.6 | convolution fusion | flops 404226048 | bytes 11010240 | tf_op jit(solution)/shard_map/rjab,prjb->pra/dot_general | solution.py:40
  176.4 17.2 %all-to-all-done.1 = bf16[64,64,3,128]{3,0,2,1:T(8,128)(2,1)S(1)} async-done(((bf16[64,64,3,128]{3,0,2,1:T(8,128)(2,1)}), bf16[64,64,3,128]{3,0,2,1:T(8,128)(2,1)S(1)}, u32[]{:S(2)}, u32[]{:S(2)}) %all-to-all-start.1) | async-done | bytes 3145760 | tf_op jit(solution)/shard_map/all_to_all | solution.py:23
  193.7 1.9 gather_fusion.5
  195.6 4.2 %fusion.18 = f32[48,8,8,128]{3,2,1,0:T(8,128)S(1)} fusion(f32[48,64,128,1]{2,1,3,0:T(8,128)} %fusion, bf16[48,6,128,128]{3,2,1,0:T(8,128)(2,1)} %param.12, bf16[48,2,64,128]{3,2,1,0:T(8,128)(2,1)} %bitcast.81, pred[48,2]{1,0:T(8,128)(4,1)S(1)} %copy.50), kind=kOutput, calls=%fused_computation.31 | convolution fusion | flops 202899456 | bytes 7864416 | tf_op jit(solution)/shard_map/rjab,prjb->pra/dot_general | solution.py:46
  199.8 0.6 fusion.14
  200.5 0.7 pad_maximum_fusion
  (26 shorter events, 0.4 us)
Async XLA Ops:
  9.3 3.9 %copy-start = (bf16[64,48,128]{2,0,1:T(8,128)(2,1)}, bf16[64,48,128]{2,0,1:T(8,128)(2,1)S(1)}, u32[]{:S(2)}) copy-start(bf16[64,48,128]{2,0,1:T(8,128)(2,1)S(1)} %copy_bitcast_fusion) | copy-start | bytes 2359300
  16.5 12.8 %copy-start.5 = (s32[48,2]{0,1:T(2,128)S(1)}, s32[48,2]{0,1:T(2,128)}, u32[]{:S(2)}) copy-start(s32[48,2]{0,1:T(2,128)} %param.14) | copy-start | bytes 1156
  16.5 13.1 %copy-start.4 = (s32[48,4]{0,1:T(4,128)S(1)}, s32[48,4]{0,1:T(4,128)}, u32[]{:S(2)}) copy-start(s32[48,4]{0,1:T(4,128)} %param.13) | copy-start | bytes 2308
  16.5 85.9 %all-to-all-start = ((bf16[64,64,3,128]{3,0,2,1:T(8,128)(2,1)}), bf16[64,64,3,128]{3,0,2,1:T(8,128)(2,1)S(1)}, u32[]{:S(2)}, u32[]{:S(2)}) async-start(bf16[64,64,3,128]{3,0,2,1:T(8,128)(2,1)} %bitcast_select_fusion.1), calls=%async_computation | async-start | bytes 6291456 | tf_op jit(solution)/shard_map/all_to_all | solution.py:23
  28.5 44.8 %all-gather.3.cloned.1.call-start = ((), (), s32[]{:S(2)}) async-start(), calls=%async_computation.2 | async-start | bytes 3932160 | tf_op jit(solution)/shard_map/all_gather | solution.py:38
  108.4 2.8 %copy-start.1 = (bf16[64,48,128]{2,0,1:T(8,128)(2,1)}, bf16[64,48,128]{2,0,1:T(8,128)(2,1)S(1)}, u32[]{:S(2)}) copy-start(bf16[64,48,128]{2,0,1:T(8,128)(2,1)S(1)} %fusion.36) | copy-start | bytes 2359300
  114.5 79.1 %all-to-all-start.1 = ((bf16[64,64,3,128]{3,0,2,1:T(8,128)(2,1)}), bf16[64,64,3,128]{3,0,2,1:T(8,128)(2,1)S(1)}, u32[]{:S(2)}, u32[]{:S(2)}) async-start(bf16[64,64,3,128]{3,0,2,1:T(8,128)(2,1)} %bitcast_select_fusion), calls=%async_computation.1 | async-start | bytes 6291456 | tf_op jit(solution)/shard_map/all_to_all | solution.py:23
  119.8 44.8 %all-gather.5.cloned.1.call-start = ((), (), s32[]{:S(2)}) async-start(), calls=%async_computation.3 | async-start | bytes 3932160 | tf_op jit(solution)/shard_map/all_gather | solution.py:38
  195.6 4.2 %copy-start.2 = (bf16[64,48,128]{2,0,1:T(8,128)(2,1)S(1)}, bf16[64,48,128]{2,0,1:T(8,128)(2,1)}, u32[]{:S(2)}) copy-start(bf16[64,48,128]{2,0,1:T(8,128)(2,1)} %copy-done.1) | copy-start | bytes 2359300
  195.6 4.2 %copy-start.3 = (bf16[64,6144]{1,0:T(8,128)(2,1)S(1)}, bf16[64,6144]{1,0:T(8,128)(2,1)}, u32[]{:S(2)}) copy-start(bf16[64,6144]{1,0:T(8,128)(2,1)} %param.17) | copy-start | bytes 2359300
Sparse Core Ops, SparseCore 0:
  31.2 42.0 all-gather.2
  122.4 42.0 all-gather.4
where the time goes:
time: 208 us
  waiting for transfers between devices  123 us (59%)
  matrix products  22.7 us (11%)
  local copies, waits for them, and re-layouts  21 us (10%)
  starting transfers between devices  17.4 us (8%)
  between operations  13.6 us (7%)
  other arithmetic  10.1 us (5%)
    all_gather x2, waiting for transfers between devices, local_part(): panel_all = lax.all_gather(own, 'grp', axis=1, tiled=True)  87.3 us
    all_to_all x2, waiting for transfers between devices, send_boundary(): lax.all_to_all(outgoing, 'dom', split_axis=1, concat_axis=1, tiled=True)  34.4 us
    all_to_all x2, starting transfers between devices, send_boundary(): lax.all_to_all(outgoing, 'dom', split_axis=1, concat_axis=1, tiled=True)  17.3 us
    dot_general x2, matrix products, local_part(): jnp.einsum('rjab,prjb->pra', local_blocks, picked, preferred_element_type...  14.5 us
    gather x2, local copies, waits for them, and re-layouts, local_part(): picked = jnp.take(panel_all, local_cols, axis=1)  9.29 us
    dot_general x2, matrix products, remote_part(): jnp.einsum('rjab,prjb->pra', remote_blocks, picked, preferred_element_typ...  8.29 us
    select_n x2, other arithmetic, send_boundary(): jnp.where(live[None, :, :, None], outgoing, jnp.zeros_like(outgoing))  6.68 us
    gather x2, local copies, waits for them, and re-layouts, send_boundary(): outgoing = jnp.take(own, send_list, axis=1)  5.5 us
  transfers between devices with their start and end apart: 4, of which 4 were waited for; matrix products, arithmetic and copies ran while one was open for 12% of the time, Pallas kernels for 0%

commit v1 on v0

v1 whole, which is shorter than its diff:
```python
import functools
import math

import jax
import jax.numpy as jnp
from jax import lax
from jax.experimental import pallas as pl
from jax.experimental.pallas import tpu as pltpu
from jax.sharding import PartitionSpec as P

PROBES = 64
LOCAL = 4
REMOTE = 2
KMOM = 256
LANES = 4
STEP = 8


def grant(mib):
    return pltpu.CompilerParams(vmem_limit_bytes=mib * 1024 * 1024)


HBM = pl.BlockSpec(memory_space=pltpu.HBM)
VMEM = pl.BlockSpec(memory_space=pltpu.VMEM)
SMEM = pl.BlockSpec(memory_space=pltpu.SMEM)
DMA = pltpu.SemaphoreType.DMA


def jackson(order, total):
    angle = math.pi / (total + 1)
    return (
        (total - order + 1) * math.cos(order * angle) + math.sin(order * angle) / math.tan(angle)
    ) / (total + 1)


def pair_dot(fields, mats):
    left = jnp.concatenate(fields, axis=1)
    right = jnp.concatenate(mats, axis=1)
    return lax.dot_general(left, right, (((1,), (1,)), ((), ())), preferred_element_type=jnp.float32)


def start_sends(table_ref, count_ref, src_ref, send_ref, sem):
    rows = src_ref.shape[0] - 1
    peers, slots = send_ref.shape[0], send_ref.shape[1]

    @pl.loop(0, peers, unroll=4)
    def _(d):
        count = count_ref[d]
        for s in range(slots):
            index = jnp.where(s < count, table_ref[s, 0, d], rows)
            pltpu.make_async_copy(src_ref.at[index], send_ref.at[d, s], sem).start()


def wait_sends(send_ref, sem):
    pltpu.make_async_copy(send_ref, send_ref, sem).wait()


def pack_kernel(table_ref, count_ref, probes_ref, own_ref, send_ref, src_ref, own_sem, send_sem):
    rows, _, size = own_ref.shape
    for r in range(rows):
        src_ref[r] = probes_ref[:, r * size:(r + 1) * size]
    src_ref[rows] = jnp.zeros_like(src_ref[rows])
    start_sends(table_ref, count_ref, src_ref, send_ref, send_sem)
    own = pltpu.make_async_copy(src_ref.at[pl.ds(0, rows)], own_ref, own_sem)
    own.start()
    own.wait()
    wait_sends(send_ref, send_sem)


def pack(table, counts, probes, peers, slots, rows, size):
    part = probes.shape[0]
    return pl.pallas_call(
        pack_kernel,
        in_specs=[SMEM, SMEM, VMEM],
        out_specs=[HBM, HBM],
        scratch_shapes=[pltpu.VMEM((rows + 1, part, size), probes.dtype), DMA, DMA],
        out_shape=[pltpu.HBM((rows, part, size), probes.dtype), pltpu.HBM((peers, slots, part, size), probes.dtype)],
        compiler_params=grant(62),
        name="pack",
    )(table, counts, probes)


def block_copy(blocks_ref, held_ref, sem, first, count, step):
    rows = pl.ds(step * STEP, STEP)
    return pltpu.make_async_copy(blocks_ref.at[rows, pl.ds(first, count)], held_ref.at[rows], sem.at[step])


def local_products(lane_ref, pieces, blocks_ref, panel_ref, held_ref, panel_sem, sem, cols_ref, use):
    rows = pieces[0].shape[0]
    steps = rows // STEP
    me = lane_ref[0]
    copies = []
    for shift, piece in enumerate(pieces):
        lane = lax.rem(me + LANES - shift, LANES)
        copies.append(pltpu.make_async_copy(piece, panel_ref.at[pl.ds(lane * rows, rows)], panel_sem.at[shift]))
    for copy in copies:
        copy.start()
    for step in range(steps):
        block_copy(blocks_ref, held_ref, sem, 0, LOCAL, step).start()
    for copy in copies:
        copy.wait()

    @pl.loop(0, steps)
    def _(step):
        block_copy(blocks_ref, held_ref, sem, 0, LOCAL, step).wait()
        for t in range(STEP):
            r = step * STEP + t
            total = None
            for j in range(0, LOCAL, 2):
                term = pair_dot(
                    [panel_ref[cols_ref[j + k, r]] for k in range(2)],
                    [held_ref[r, j + k] for k in range(2)],
                )
                total = term if total is None else total + term
            use(r, total)


def local_kernel(cols_ref, lane_ref, own_ref, prev_ref, across_ref, next_ref, blocks_ref, sum_ref, panel_ref, held_ref, panel_sem, sem):
    def use(r, total):
        sum_ref[r] = total

    local_products(
        lane_ref, (own_ref, prev_ref, across_ref, next_ref), blocks_ref, panel_ref, held_ref, panel_sem, sem, cols_ref, use
    )


def local_scratch(rows, part, size, kind):
    return [
        pltpu.VMEM((LANES * rows, part, size), kind),
        pltpu.VMEM((rows, LOCAL, size, size), kind),
        DMA((LANES,)),
        DMA((rows // STEP,)),
    ]


def in_hbm(x):
    return pltpu.with_memory_space_constraint(x, pltpu.HBM)


def in_vmem(x):
    return pltpu.with_memory_space_constraint(x, pltpu.VMEM)


def local_part(cols, lane, pieces, blocks):
    rows, part, size = pieces[0].shape
    return pl.pallas_call(
        local_kernel,
        in_specs=[SMEM, SMEM] + [HBM] * 5,
        out_specs=VMEM,
        scratch_shapes=local_scratch(rows, part, size, blocks.dtype),
        out_shape=jax.ShapeDtypeStruct((rows, part, size), jnp.float32),
        compiler_params=grant(24),
        name="local",
    )(cols, lane, *[in_hbm(x) for x in pieces], in_hbm(blocks))


def remote_products(refs_ref, got_ref, blocks_ref, other_ref, far_ref, near_ref, far_sem, near_sem, use):
    rows = near_ref.shape[0]
    steps = rows // STEP

    def near_copy(step):
        at = pl.ds(step * STEP, STEP)
        return pltpu.make_async_copy(other_ref.at[at], near_ref.at[at], near_sem.at[step])

    for step in range(steps):
        block_copy(blocks_ref, far_ref, far_sem, LOCAL, REMOTE, step).start()
        near_copy(step).start()

    @pl.loop(0, steps)
    def _(step):
        block_copy(blocks_ref, far_ref, far_sem, LOCAL, REMOTE, step).wait()
        near_copy(step).wait()
        for t in range(STEP):
            r = step * STEP + t
            total = pair_dot(
                [got_ref[refs_ref[j, r]] for j in range(REMOTE)],
                [far_ref[r, j] for j in range(REMOTE)],
            )
            use(r, total, near_ref[r])


def remote_scratch(rows, part, size, kind, near_kind):
    return [
        pltpu.VMEM((rows, REMOTE, size, size), kind),
        pltpu.VMEM((rows, part, size), near_kind),
        DMA((rows // STEP,)),
        DMA((rows // STEP,)),
    ]


def first_kernel(refs_ref, table_ref, count_ref, got_ref, sum_ref, blocks_ref, own_ref, send_ref, src_ref, own_sem, send_sem, *scratch):
    rows = own_ref.shape[0]
    src_ref[rows] = jnp.zeros_like(src_ref[rows])

    def use(r, total, near):
        src_ref[r] = (near + total).astype(src_ref.dtype)

    remote_products(refs_ref, got_ref, blocks_ref, sum_ref, *scratch, use)
    start_sends(table_ref, count_ref, src_ref, send_ref, send_sem)
    own = pltpu.make_async_copy(src_ref.at[pl.ds(0, rows)], own_ref, own_sem)
    own.start()
    own.wait()
    wait_sends(send_ref, send_sem)


def first_part(refs, table, counts, got, sums, blocks, peers, slots):
    rows, part, size = sums.shape
    return pl.pallas_call(
        first_kernel,
        in_specs=[SMEM, SMEM, SMEM, VMEM, HBM, HBM],
        out_specs=[HBM, HBM],
        scratch_shapes=[pltpu.VMEM((rows + 1, part, size), got.dtype), DMA, DMA]
        + remote_scratch(rows, part, size, blocks.dtype, sums.dtype),
        out_shape=[pltpu.HBM((rows, part, size), got.dtype), pltpu.HBM((peers, slots, part, size), got.dtype)],
        compiler_params=grant(24),
        name="first",
    )(refs, table, counts, in_vmem(got), in_hbm(sums), in_hbm(blocks))


def near_kernel(cols_ref, lane_ref, own_ref, prev_ref, across_ref, next_ref, blocks_ref, probes_ref, near_ref, base_ref, panel_ref, held_ref, base_sem, panel_sem, sem):
    rows, _, size = base_ref.shape
    copy = pltpu.make_async_copy(probes_ref, base_ref, base_sem)
    copy.start()
    copy.wait()
    me = lane_ref[0]

    def use(r, total):
        base = base_ref[r].astype(jnp.float32)
        one = panel_ref[me * rows + r].astype(jnp.float32)
        at = pl.ds(pl.multiple_of(r * size, size), size)
        for k, other in enumerate((base, one, 2.0 * total - base)):
            near_ref[k:k + 1, at] = jnp.sum(base * other, axis=0, keepdims=True)

    local_products(
        lane_ref, (own_ref, prev_ref, across_ref, next_ref), blocks_ref, panel_ref, held_ref, panel_sem, sem, cols_ref, use
    )


def near_part(cols, lane, pieces, blocks, base):
    rows, part, size = pieces[0].shape
    panel, held, panel_sem, sem = local_scratch(rows, part, size, blocks.dtype)
    return pl.pallas_call(
        near_kernel,
        in_specs=[SMEM, SMEM] + [HBM] * 6,
        out_specs=VMEM,
        scratch_shapes=[pltpu.VMEM(base.shape, base.dtype), panel, held, DMA, panel_sem, sem],
        out_shape=jax.ShapeDtypeStruct((3, rows * size), jnp.float32),
        compiler_params=grant(24),
        name="near",
    )(cols, lane, *[in_hbm(x) for x in pieces], in_hbm(blocks), in_hbm(base))


def moments_kernel(scale, refs_ref, got_ref, near_ref, base_ref, blocks_ref, out_ref, *scratch):
    out_ref[0:1] = near_ref[0:1] * scale[0]
    out_ref[1:2] = near_ref[1:2] * scale[1]
    size = base_ref.shape[2]

    def use(r, total, base):
        at = pl.ds(pl.multiple_of(r * size, size), size)
        value = near_ref[2:3, at] + 2.0 * jnp.sum(total * base.astype(jnp.float32), axis=0, keepdims=True)
        out_ref[2:3, at] = value * scale[2]

    remote_products(refs_ref, got_ref, blocks_ref, base_ref, *scratch, use)


def moments_part(refs, got, near, base, blocks, scale):
    rows, part, size = base.shape
    return pl.pallas_call(
        functools.partial(moments_kernel, scale),
        in_specs=[SMEM, VMEM, VMEM, HBM, HBM],
        out_specs=VMEM,
        scratch_shapes=remote_scratch(rows, part, size, blocks.dtype, base.dtype),
        out_shape=jax.ShapeDtypeStruct(near.shape, near.dtype),
        compiler_params=grant(24),
        name="moments",
    )(refs, in_vmem(got), near, in_hbm(base), in_hbm(blocks))


def on_device(blocks, local_cols, remote_refs, send_blocks, send_counts, probes):
    rows, _, size, _ = blocks.shape
    peers, slots = send_blocks.shape[2], send_blocks.shape[3]
    table = send_blocks.transpose(0, 3, 1, 2)[0]
    counts = send_counts[0, 0]
    cols = local_cols.T
    refs = remote_refs.T
    lane = lax.axis_index("grp").astype(jnp.int32).reshape(1)
    norm = 1.0 / math.sqrt(PROBES)
    scale = (
        jackson(0, KMOM) * norm,
        2.0 * jackson(1, KMOM) * norm,
        2.0 * jackson(2, KMOM) * norm,
    )

    def exchange(send):
        got = lax.all_to_all(send, "dom", split_axis=0, concat_axis=0, tiled=True)
        return got.reshape(peers * slots, send.shape[2], size)

    def panel(own):
        pieces = [own]
        for shift in (1, 2, 3):
            pieces.append(lax.ppermute(own, "grp", [(i, (i + shift) % LANES) for i in range(LANES)]))
        return pieces

    base, send = pack(table, counts, probes, peers, slots, rows, size)
    got = exchange(send)
    sums = local_part(cols, lane, panel(base), blocks)
    first, send = first_part(refs, table, counts, got, sums, blocks, peers, slots)
    got = exchange(send)
    near = near_part(cols, lane, panel(first), blocks, base)
    return moments_part(refs, got, near, base, blocks, scale)


def solution(mesh):
    in_specs = (
        P(("dom", "grp"), None, None, None),
        P(("dom", "grp"), None),
        P(("dom", "grp"), None),
        P("dom", "grp", None, None),
        P("dom", "grp", None),
        P(None, ("dom", "grp")),
    )
    out_specs = P(None, ("dom", "grp"))
    return jax.shard_map(
        on_device, mesh=mesh, in_specs=in_specs, out_specs=out_specs, check_vma=False
    )
```

time: 208 us -> 178 us (0.86)
  Pallas kernels: 0 us -> 28.5 us
  matrix products: 22.7 us -> 0 us
  local copies, waits for them, and re-layouts: 21 us -> 2.08 us
  between operations: 13.6 us -> 0.09 us
  other arithmetic: 10.1 us -> 0 us
  starting transfers between devices: 17.4 us -> 24.1 us
    all_gather x2 -> x0, waiting for transfers between devices: 87.3 us -> none  [local_part(): panel_all = lax.all_gather(own, 'grp', axis=1, tiled=True)]
    ppermute x0 -> x6, waiting for transfers between devices: none -> 69.9 us  [panel(): lax.ppermute(own, 'grp', [(i, (i + shift) % LANES) for i in range(LANES)])]
    pallas_call x0 -> x5, Pallas kernels: none -> 28.5 us  [the longest x1 8.39 us: near_part(): pl.pallas_call(near_kernel, in_specs=[SMEM, SMEM] + [HBM] * 6, out_specs=...]
    dot_general x4 -> x0, matrix products: 22.7 us -> none  [the longest x2 14.5 us: local_part(): jnp.einsum('rjab,prjb->pra', local_blocks, picked, preferred_element_type...]
    all_to_all x2, waiting for transfers between devices: 34.4 us -> 53.3 us  [exchange(): got = lax.all_to_all(send, 'dom', split_axis=0, concat_axis=0, tiled=True)]
    gather x6 -> x0, local copies, waits for them, and re-layouts: 18.7 us -> none  [the longest x2 9.29 us: local_part(): picked = jnp.take(panel_all, local_cols, axis=1)]
    select_n x5 -> x0, other arithmetic: 7.37 us -> none  [the longest x2 6.68 us: send_boundary(): jnp.where(live[None, :, :, None], outgoing, jnp.zeros_like(outgoing))]
    ppermute x0 -> x6, starting transfers between devices: none -> 6.86 us  [panel(): lax.ppermute(own, 'grp', [(i, (i + shift) % LANES) for i in range(LANES)])]
  transfers between devices with their start and end apart: 4 -> 8, of which waited for: 4 -> 8; matrix products, arithmetic and copies ran while one was open for 12% -> 0% of each run, Pallas kernels for 0% -> 9%
where the time goes in v1:
time: 178 us
  waiting for transfers between devices  123 us (69%)
  Pallas kernels  28.5 us (16%)
  starting transfers between devices  24.1 us (14%)
  local copies, waits for them, and re-layouts  2.08 us (1%)
    ppermute x6, waiting for transfers between devices, panel(): lax.ppermute(own, 'grp', [(i, (i + shift) % LANES) for i in range(LANES)])  69.9 us
    all_to_all x2, waiting for transfers between devices, exchange(): got = lax.all_to_all(send, 'dom', split_axis=0, concat_axis=0, tiled=True)  53.3 us
    all_to_all x2, starting transfers between devices, exchange(): got = lax.all_to_all(send, 'dom', split_axis=0, concat_axis=0, tiled=True)  17.2 us
    pallas_call x1, Pallas kernels, near_part(): pl.pallas_call(near_kernel, in_specs=[SMEM, SMEM] + [HBM] * 6, out_specs=...  8.39 us
    pallas_call x1, Pallas kernels, local_part(): pl.pallas_call(local_kernel, in_specs=[SMEM, SMEM] + [HBM] * 5, out_specs...  7.19 us
    ppermute x6, starting transfers between devices, panel(): lax.ppermute(own, 'grp', [(i, (i + shift) % LANES) for i in range(LANES)])  6.86 us
    pallas_call x1, Pallas kernels, first_part(): pl.pallas_call(first_kernel, in_specs=[SMEM, SMEM, SMEM, VMEM, HBM, HBM],...  5.49 us
    pallas_call x1, Pallas kernels, moments_part(): pl.pallas_call(functools.partial(moments_kernel, scale), in_specs=[SMEM,...  4.28 us
  transfers between devices with their start and end apart: 8, of which 8 were waited for; matrix products, arithmetic and copies ran while one was open for 0% of the time, Pallas kernels for 9%

profile of v1, /device:TPU:16, one launch (start us, length us, event | category | flops | bytes accessed | tf_op | source)
XLA Modules:
  0.0 178.0 jit_solution(1021631999790272044)
XLA Ops:
  0.0 3.2 %pack.1 = (bf16[48,64,128]{2,1,0:T(8,128)(2,1)}, bf16[64,3,64,128]{3,2,1,0:T(8,128)(2,1)}) custom-call(s32[3,1,64]{2,1,0:T(1,128)} %bitcast.13, s32[64]{0:T(128)} %bitcast.17, bf16[64,6144]{1,0:T(8,128)(2,1)} %probes_ref.1), custom_call_target="tpu_custom_call" | custom-call | tf_op jit(solution)/shard_map/pack/pallas_call | solution.py:72
  3.2 0.0 copy-start.1
  3.2 11.9 %all-to-all-start = ((bf16[64,3,64,128]{3,2,1,0:T(8,128)(2,1)}), bf16[64,3,64,128]{3,2,1,0:T(8,128)(2,1)S(1)}, u32[]{:S(2)}, u32[]{:S(2)}) async-start(bf16[64,3,64,128]{3,2,1,0:T(8,128)(2,1)} %get-tuple-element.9), calls=%async_computation | async-start | bytes 6291456 | tf_op jit(solution)/shard_map/all_to_all | solution.py:295
  15.2 0.5 collective-permute-start.2
  15.7 2.9 %collective-permute-start.1 = (bf16[48,64,128]{2,1,0:T(8,128)(2,1)}, bf16[48,64,128]{2,1,0:T(8,128)(2,1)}, u32[]{:S(2)}, u32[]{:S(2)}) collective-permute-start(bf16[48,64,128]{2,1,0:T(8,128)(2,1)} %get-tuple-element.10.own_ref.probes_ref.base_ref), channel_id=1, source_target_pairs={{0,2},{1,3},{2,0},{3,1},{4,6},{5,7},{6,4},{7,5},{8,10},{9,11},{10,... | collective-permute-start | bytes 2359304 | tf_op jit(solution)/shard_map/ppermute | solution.py:301
  18.6 0.0 collective-permute-start
  18.6 17.4 %collective-permute-done.2.next_ref = bf16[48,64,128]{2,1,0:T(8,128)(2,1)} collective-permute-done((bf16[48,64,128]{2,1,0:T(8,128)(2,1)}, bf16[48,64,128]{2,1,0:T(8,128)(2,1)}, u32[]{:S(2)}, u32[]{:S(2)}) %collective-permute-start.2) | collective-permute-done | bytes 786464 | tf_op jit(solution)/shard_map/ppermute | solution.py:301
  36.0 2.0 %collective-permute-done.1.across_ref = bf16[48,64,128]{2,1,0:T(8,128)(2,1)} collective-permute-done((bf16[48,64,128]{2,1,0:T(8,128)(2,1)}, bf16[48,64,128]{2,1,0:T(8,128)(2,1)}, u32[]{:S(2)}, u32[]{:S(2)}) %collective-permute-start.1) | collective-permute-done | bytes 786464 | tf_op jit(solution)/shard_map/ppermute | solution.py:301
  38.0 15.6 %collective-permute-done.prev_ref = bf16[48,64,128]{2,1,0:T(8,128)(2,1)} collective-permute-done((bf16[48,64,128]{2,1,0:T(8,128)(2,1)}, bf16[48,64,128]{2,1,0:T(8,128)(2,1)}, u32[]{:S(2)}, u32[]{:S(2)}) %collective-permute-start) | collective-permute-done | bytes 786464 | tf_op jit(solution)/shard_map/ppermute | solution.py:301
  53.6 0.0 copy-done.1
  53.6 0.0 copy-start.2
  53.6 7.2 %local.1.sum_ref = f32[48,64,128]{2,1,0:T(8,128)S(1)} custom-call(s32[4,48]{1,0:T(4,128)S(1)} %bitcast.11, s32[1]{0:T(128)} %bitcast.7.lane_ref, bf16[48,64,128]{2,1,0:T(8,128)(2,1)} %get-tuple-element.10.own_ref.probes_ref.base_ref, bf16[48,64,128]{2,1,0:T(8,128)(2,1)} %collective-permute-done.prev_ref, ...), custom_call_target="tpu_custom_call" | custom-call | tf_op jit(solution)/shard_map/local/pallas_call | solution.py:146
  60.8 0.0 copy-start
  60.8 1.1 copy-done
  62.0 27.1 %all-to-all-done = bf16[64,3,64,128]{3,2,1,0:T(8,128)(2,1)S(1)} async-done(((bf16[64,3,64,128]{3,2,1,0:T(8,128)(2,1)}), bf16[64,3,64,128]{3,2,1,0:T(8,128)(2,1)S(1)}, u32[]{:S(2)}, u32[]{:S(2)}) %all-to-all-start) | async-done | bytes 3145760 | tf_op jit(solution)/shard_map/all_to_all | solution.py:295
  89.0 0.0 copy-done.2
  89.0 0.0 copy-done.3
  89.0 0.0 copy-done.4
  89.0 5.5 %first.1 = (bf16[48,64,128]{2,1,0:T(8,128)(2,1)}, bf16[64,3,64,128]{3,2,1,0:T(8,128)(2,1)}) custom-call(s32[2,48]{1,0:T(2,128)S(1)} %bitcast.15, s32[3,1,64]{2,1,0:T(1,128)S(1)} %bitcast.14, s32[64]{0:T(128)S(1)} %bitcast.18, bf16[192,64,128]{2,1,0:T(8,128)(2,1)S(1)} %bitcast.10, f32[48,64,128]{2,1,0:T(8,128)} %copy-done, bf16[48,6,128,128]{3,2,1,0:T(8,128)(2,1)} %blocks_ref.7), custom_call_target="tpu_custom_call" | custom-call | tf_op jit(solution)/shard_map/first/pallas_call | solution.py:208
  94.5 5.3 %all-to-all-start.1 = ((bf16[64,3,64,128]{3,2,1,0:T(8,128)(2,1)}), bf16[64,3,64,128]{3,2,1,0:T(8,128)(2,1)S(1)}, u32[]{:S(2)}, u32[]{:S(2)}) async-start(bf16[64,3,64,128]{3,2,1,0:T(8,128)(2,1)} %get-tuple-element.11), calls=%async_computation.1 | async-start | bytes 6291456 | tf_op jit(solution)/shard_map/all_to_all | solution.py:295
  99.8 0.5 collective-permute-start.5
  100.4 2.9 %collective-permute-start.4 = (bf16[48,64,128]{2,1,0:T(8,128)(2,1)}, bf16[48,64,128]{2,1,0:T(8,128)(2,1)S(1)}, u32[]{:S(2)}, u32[]{:S(2)}) collective-permute-start(bf16[48,64,128]{2,1,0:T(8,128)(2,1)} %get-tuple-element.12.own_ref), channel_id=1, source_target_pairs={{0,2},{1,3},{2,0},{3,1},{4,6},{5,7},{6,4},{7,5},{8,10},{9,11},{10,... | collective-permute-start | bytes 2359304 | tf_op jit(solution)/shard_map/ppermute | solution.py:301
  103.3 0.0 collective-permute-start.3
  103.3 17.3 %collective-permute-done.5.next_ref = bf16[48,64,128]{2,1,0:T(8,128)(2,1)S(1)} collective-permute-done((bf16[48,64,128]{2,1,0:T(8,128)(2,1)}, bf16[48,64,128]{2,1,0:T(8,128)(2,1)S(1)}, u32[]{:S(2)}, u32[]{:S(2)}) %collective-permute-start.5) | collective-permute-done | bytes 786464 | tf_op jit(solution)/shard_map/ppermute | solution.py:301
  120.5 2.0 %collective-permute-done.4.across_ref = bf16[48,64,128]{2,1,0:T(8,128)(2,1)S(1)} collective-permute-done((bf16[48,64,128]{2,1,0:T(8,128)(2,1)}, bf16[48,64,128]{2,1,0:T(8,128)(2,1)S(1)}, u32[]{:S(2)}, u32[]{:S(2)}) %collective-permute-start.4) | collective-permute-done | bytes 786464 | tf_op jit(solution)/shard_map/ppermute | solution.py:301
  122.5 15.6 %collective-permute-done.3.prev_ref = bf16[48,64,128]{2,1,0:T(8,128)(2,1)S(1)} collective-permute-done((bf16[48,64,128]{2,1,0:T(8,128)(2,1)}, bf16[48,64,128]{2,1,0:T(8,128)(2,1)S(1)}, u32[]{:S(2)}, u32[]{:S(2)}) %collective-permute-start.3) | collective-permute-done | bytes 786464 | tf_op jit(solution)/shard_map/ppermute | solution.py:301
  138.1 0.0 copy-done.5
  138.1 0.0 copy-done.6
  138.2 0.9 copy-done.7
  139.1 8.4 %near.1.near_ref = f32[3,6144]{1,0:T(4,128)S(1)} custom-call(s32[4,48]{1,0:T(4,128)S(1)} %bitcast.12, s32[1]{0:T(128)} %bitcast.7.lane_ref, bf16[48,64,128]{2,1,0:T(8,128)(2,1)} %get-tuple-element.12.own_ref, bf16[48,64,128]{2,1,0:T(8,128)(2,1)} %copy-done.7, bf16[48,64,128]{2,1,0:T(8,128)(2,1)} %copy-done.6, bf16[48,64,128]{2,1,0:T(8,128)(2,1)} %copy-done.5, ...), custom_call_target="tpu_custom_call" | custom-call | tf_op jit(solution)/shard_map/near/pallas_call | solution.py:242
  147.5 26.2 %all-to-all-done.1 = bf16[64,3,64,128]{3,2,1,0:T(8,128)(2,1)S(1)} async-done(((bf16[64,3,64,128]{3,2,1,0:T(8,128)(2,1)}), bf16[64,3,64,128]{3,2,1,0:T(8,128)(2,1)S(1)}, u32[]{:S(2)}, u32[]{:S(2)}) %all-to-all-start.1) | async-done | bytes 3145760 | tf_op jit(solution)/shard_map/all_to_all | solution.py:295
  173.7 4.3 %moments.1 = f32[3,6144]{1,0:T(4,128)} custom-call(s32[2,48]{1,0:T(2,128)S(1)} %bitcast.16, bf16[192,64,128]{2,1,0:T(8,128)(2,1)S(1)} %bitcast.9, f32[3,6144]{1,0:T(4,128)S(1)} %near.1.near_ref, bf16[48,64,128]{2,1,0:T(8,128)(2,1)} %get-tuple-element.10.own_ref.probes_ref.base_ref, bf16[48,6,128,128]{3,2,1,0:T(8,128)(2,1)} %blocks_ref.7), custom_call_target="tpu_custom_call" | custom-call | tf_op jit(solution)/shard_map/moments/pallas_call | solution.py:268
  (5 shorter events, 0.0 us)
Async XLA Ops:
  3.2 50.4 %copy-start.1 = (s32[48,4]{0,1:T(4,128)S(1)}, s32[48,4]{0,1:T(4,128)}, u32[]{:S(2)}) copy-start(s32[48,4]{0,1:T(4,128)} %param.7) | copy-start | bytes 2308
  3.2 85.8 %all-to-all-start = ((bf16[64,3,64,128]{3,2,1,0:T(8,128)(2,1)}), bf16[64,3,64,128]{3,2,1,0:T(8,128)(2,1)S(1)}, u32[]{:S(2)}, u32[]{:S(2)}) async-start(bf16[64,3,64,128]{3,2,1,0:T(8,128)(2,1)} %get-tuple-element.9), calls=%async_computation | async-start | bytes 6291456 | tf_op jit(solution)/shard_map/all_to_all | solution.py:295
  15.2 20.8 %collective-permute-start.2 = (bf16[48,64,128]{2,1,0:T(8,128)(2,1)}, bf16[48,64,128]{2,1,0:T(8,128)(2,1)}, u32[]{:S(2)}, u32[]{:S(2)}) collective-permute-start(bf16[48,64,128]{2,1,0:T(8,128)(2,1)} %get-tuple-element.10.own_ref.probes_ref.base_ref), channel_id=1, source_target_pairs={{0,3},{1,0},{2,1},{3,2},{4,7},{5,4},{6,5},{7,6},{8,11},{9,8},{10,9... | collective-permute-start | bytes 2359304 | tf_op jit(solution)/shard_map/ppermute | solution.py:301
  15.7 22.3 %collective-permute-start.1 = (bf16[48,64,128]{2,1,0:T(8,128)(2,1)}, bf16[48,64,128]{2,1,0:T(8,128)(2,1)}, u32[]{:S(2)}, u32[]{:S(2)}) collective-permute-start(bf16[48,64,128]{2,1,0:T(8,128)(2,1)} %get-tuple-element.10.own_ref.probes_ref.base_ref), channel_id=1, source_target_pairs={{0,2},{1,3},{2,0},{3,1},{4,6},{5,7},{6,4},{7,5},{8,10},{9,11},{10,... | collective-permute-start | bytes 2359304 | tf_op jit(solution)/shard_map/ppermute | solution.py:301
  18.6 35.0 %collective-permute-start = (bf16[48,64,128]{2,1,0:T(8,128)(2,1)}, bf16[48,64,128]{2,1,0:T(8,128)(2,1)}, u32[]{:S(2)}, u32[]{:S(2)}) collective-permute-start(bf16[48,64,128]{2,1,0:T(8,128)(2,1)} %get-tuple-element.10.own_ref.probes_ref.base_ref), channel_id=1, source_target_pairs={{0,1},{1,2},{2,3},{3,0},{4,5},{5,6},{6,7},{7,4},{8,9},{9,10},{10,1... | collective-permute-start | bytes 2359304 | tf_op jit(solution)/shard_map/ppermute | solution.py:301
  53.6 35.4 %copy-start.2 = (s32[1,1,64,3]{2,1,3,0:T(1,128)S(1)}, s32[1,1,64,3]{2,1,3,0:T(1,128)}, u32[]{:S(2)}) copy-start(s32[1,1,64,3]{2,1,3,0:T(1,128)} %param.9) | copy-start | bytes 2308
  53.6 35.4 %copy-start.3 = (s32[48,2]{0,1:T(2,128)S(1)}, s32[48,2]{0,1:T(2,128)}, u32[]{:S(2)}) copy-start(s32[48,2]{0,1:T(2,128)} %param.8) | copy-start | bytes 1156
  53.6 35.4 %copy-start.4 = (s32[1,1,64]{2,1,0:T(1,128)S(1)}, s32[1,1,64]{2,1,0:T(1,128)}, u32[]{:S(2)}) copy-start(s32[1,1,64]{2,1,0:T(1,128)} %param.10) | copy-start | bytes 772
  60.8 1.2 copy-start
  94.5 79.2 %all-to-all-start.1 = ((bf16[64,3,64,128]{3,2,1,0:T(8,128)(2,1)}), bf16[64,3,64,128]{3,2,1,0:T(8,128)(2,1)S(1)}, u32[]{:S(2)}, u32[]{:S(2)}) async-start(bf16[64,3,64,128]{3,2,1,0:T(8,128)(2,1)} %get-tuple-element.11), calls=%async_computation.1 | async-start | bytes 6291456 | tf_op jit(solution)/shard_map/all_to_all | solution.py:295
  99.8 20.7 %collective-permute-start.5 = (bf16[48,64,128]{2,1,0:T(8,128)(2,1)}, bf16[48,64,128]{2,1,0:T(8,128)(2,1)S(1)}, u32[]{:S(2)}, u32[]{:S(2)}) collective-permute-start(bf16[48,64,128]{2,1,0:T(8,128)(2,1)} %get-tuple-element.12.own_ref), channel_id=1, source_target_pairs={{0,3},{1,0},{2,1},{3,2},{4,7},{5,4},{6,5},{7,6},{8,11},{9,8},{10,9... | collective-permute-start | bytes 2359304 | tf_op jit(solution)/shard_map/ppermute | solution.py:301
  100.4 22.2 %collective-permute-start.4 = (bf16[48,64,128]{2,1,0:T(8,128)(2,1)}, bf16[48,64,128]{2,1,0:T(8,128)(2,1)S(1)}, u32[]{:S(2)}, u32[]{:S(2)}) collective-permute-start(bf16[48,64,128]{2,1,0:T(8,128)(2,1)} %get-tuple-element.12.own_ref), channel_id=1, source_target_pairs={{0,2},{1,3},{2,0},{3,1},{4,6},{5,7},{6,4},{7,5},{8,10},{9,11},{10,... | collective-permute-start | bytes 2359304 | tf_op jit(solution)/shard_map/ppermute | solution.py:301
  103.3 34.9 %collective-permute-start.3 = (bf16[48,64,128]{2,1,0:T(8,128)(2,1)}, bf16[48,64,128]{2,1,0:T(8,128)(2,1)S(1)}, u32[]{:S(2)}, u32[]{:S(2)}) collective-permute-start(bf16[48,64,128]{2,1,0:T(8,128)(2,1)} %get-tuple-element.12.own_ref), channel_id=1, source_target_pairs={{0,1},{1,2},{2,3},{3,0},{4,5},{5,6},{6,7},{7,4},{8,9},{9,10},{10,1... | collective-permute-start | bytes 2359304 | tf_op jit(solution)/shard_map/ppermute | solution.py:301
  120.5 17.6 %copy-start.5 = (bf16[48,64,128]{2,1,0:T(8,128)(2,1)}, bf16[48,64,128]{2,1,0:T(8,128)(2,1)S(1)}, u32[]{:S(2)}) copy-start(bf16[48,64,128]{2,1,0:T(8,128)(2,1)S(1)} %collective-permute-done.5.next_ref) | copy-start | bytes 2359300
  122.5 15.6 %copy-start.6 = (bf16[48,64,128]{2,1,0:T(8,128)(2,1)}, bf16[48,64,128]{2,1,0:T(8,128)(2,1)S(1)}, u32[]{:S(2)}) copy-start(bf16[48,64,128]{2,1,0:T(8,128)(2,1)S(1)} %collective-permute-done.4.across_ref) | copy-start | bytes 2359300
  138.2 0.9 copy-start.7

commit v2 on v1

v2 whole, which is shorter than its diff:
```python
import functools
import math

import jax
import jax.numpy as jnp
from jax import lax
from jax.experimental import pallas as pl
from jax.experimental.pallas import tpu as pltpu
from jax.sharding import PartitionSpec as P


PROBES = 64
LOCAL = 4
REMOTE = 2
KMOM = 256
LANES = 4
STEP = 8
WIDE = 48
ZS, XS, CS = 8, 4, 2
PLANE = XS * CS
EARLY, LATE = (1, 7, 2, 6), (3, 5, 4)


def grant(mib):
    return pltpu.CompilerParams(vmem_limit_bytes=mib * 1024 * 1024)


HBM = pl.BlockSpec(memory_space=pltpu.HBM)
VMEM = pl.BlockSpec(memory_space=pltpu.VMEM)
SMEM = pl.BlockSpec(memory_space=pltpu.SMEM)
DMA = pltpu.SemaphoreType.DMA


def jackson(order, total):
    angle = math.pi / (total + 1)
    return (
        (total - order + 1) * math.cos(order * angle) + math.sin(order * angle) / math.tan(angle)
    ) / (total + 1)


def pair_dot(fields, mats):
    left = jnp.concatenate(fields, axis=1)
    right = jnp.concatenate(mats, axis=1)
    return lax.dot_general(left, right, (((1,), (1,)), ((), ())), preferred_element_type=jnp.float32)


def slot_block(table_ref, count_ref, d, s, rows):
    return jnp.where(s < count_ref[d], table_ref[s, 0, d], rows)


def start_wide(table_ref, count_ref, src_ref, send_ref, sem):
    rows = src_ref.shape[0] - 1
    peers, slots, part, _ = send_ref.shape
    probes = pl.ds(0, part)

    @pl.loop(0, peers, unroll=4)
    def _(d):
        for s in range(slots):
            index = slot_block(table_ref, count_ref, d, s, rows)
            pltpu.make_async_copy(src_ref.at[index, probes], send_ref.at[d, s], sem).start()


def start_slim(first, table_ref, count_ref, me_ref, src_ref, turn_refs, sem):
    rows = src_ref.shape[0] - 1
    part = turn_refs[0].shape[1]
    slots = turn_refs[0].shape[0] // ZS
    me = me_ref[0]
    probes = pl.ds(first, part)

    @pl.loop(0, ZS)
    def _(dz):
        z = (me // PLANE + dz) & (ZS - 1)
        for k, ref in enumerate(turn_refs):
            x = (me // CS + k // CS) & (XS - 1)
            core = (me + k) & (CS - 1)
            d = z * PLANE + x * CS + core
            for s in range(slots):
                index = slot_block(table_ref, count_ref, d, s, rows)
                pltpu.make_async_copy(src_ref.at[index, probes], ref.at[dz * slots + s], sem).start()


def wait_all(refs, sem):
    for ref in refs:
        pltpu.make_async_copy(ref, ref, sem).wait()


def load_fields(probes_ref, src_ref):
    rows, size = src_ref.shape[0] - 1, src_ref.shape[2]
    for r in range(rows):
        src_ref[r] = probes_ref[:, r * size:(r + 1) * size]
    src_ref[rows] = jnp.zeros_like(src_ref[rows])


def pack_wide_kernel(table_ref, count_ref, probes_ref, send_ref, src_ref, send_sem):
    load_fields(probes_ref, src_ref)
    start_wide(table_ref, count_ref, src_ref, send_ref, send_sem)
    wait_all([send_ref], send_sem)


def pack_wide(table, counts, probes, peers, slots, rows, size):
    kind = probes.dtype
    return pl.pallas_call(
        pack_wide_kernel,
        grid=(1,),
        in_specs=[SMEM, SMEM, pl.BlockSpec((WIDE, probes.shape[1]), lambda i: (0, 0))],
        out_specs=HBM,
        scratch_shapes=[pltpu.VMEM((rows + 1, WIDE, size), kind), DMA],
        out_shape=pltpu.HBM((peers, slots, WIDE, size), kind),
        compiler_params=grant(62),
        name="pack_wide",
    )(table, counts, probes)


def pack_slim_kernel(table_ref, count_ref, me_ref, probes_ref, own_ref, *rest):
    turn_refs, (src_ref, own_sem, turn_sem) = rest[:PLANE], rest[PLANE:]
    rows = own_ref.shape[0]
    load_fields(probes_ref, src_ref)
    own = pltpu.make_async_copy(src_ref.at[pl.ds(0, rows)], own_ref, own_sem)
    own.start()
    start_slim(WIDE, table_ref, count_ref, me_ref, src_ref, turn_refs, turn_sem)
    own.wait()
    wait_all(turn_refs, turn_sem)


def slim_shapes(peers, slots, slim, size, kind):
    return [pltpu.HBM((peers // PLANE * slots, slim, size), kind)] * PLANE


def pack_slim(table, counts, me, probes, peers, slots, rows, size):
    part, kind = probes.shape[0], probes.dtype
    return pl.pallas_call(
        pack_slim_kernel,
        in_specs=[SMEM, SMEM, SMEM, VMEM],
        out_specs=[HBM] * (1 + PLANE),
        scratch_shapes=[pltpu.VMEM((rows + 1, part, size), kind), DMA, DMA],
        out_shape=[pltpu.HBM((rows, part, size), kind)] + slim_shapes(peers, slots, part - WIDE, size, kind),
        compiler_params=grant(62),
        name="pack_slim",
    )(table, counts, me, probes)


def turn_kernel(*refs):
    got, out, (held_ref, in_sem, out_sem) = refs[:PLANE], refs[PLANE + 1:-3], refs[-3:]
    slots = out[0].shape[0] // PLANE
    for k, ref in enumerate(got):
        pltpu.make_async_copy(ref, held_ref.at[k], in_sem.at[k]).start()
    for k, ref in enumerate(got):
        pltpu.make_async_copy(ref, held_ref.at[k], in_sem.at[k]).wait()
        for dz, target in enumerate(out):
            pltpu.make_async_copy(
                held_ref.at[k, pl.ds(dz * slots, slots)], target.at[pl.ds(k * slots, slots)], out_sem
            ).start()
    wait_all(out, out_sem)


def turn(got, after):
    blocks, part, size = got[0].shape
    count = blocks // ZS * PLANE
    return pl.pallas_call(
        turn_kernel,
        in_specs=[HBM] * (PLANE + 1),
        out_specs=[HBM] * ZS,
        scratch_shapes=[pltpu.VMEM((PLANE, blocks, part, size), got[0].dtype), DMA((PLANE,)), DMA],
        out_shape=[pltpu.HBM((count, part, size), got[0].dtype)] * ZS,
        compiler_params=grant(62),
        name="turn",
    )(*[in_hbm(x) for x in got], in_hbm(after))


def block_copy(blocks_ref, held_ref, sem, first, count, step):
    rows = pl.ds(step * STEP, STEP)
    return pltpu.make_async_copy(blocks_ref.at[rows, pl.ds(first, count)], held_ref.at[rows], sem.at[step])


def local_products(lane_ref, pieces, blocks_ref, panel_ref, held_ref, panel_sem, sem, cols_ref, use, done=None):
    rows = pieces[0].shape[0]
    steps = rows // STEP
    me = lane_ref[0]
    copies = []
    for n, piece in enumerate(pieces):
        lane = lax.rem(me + LANES - n % LANES, LANES)
        probes = pl.ds(n // LANES * WIDE, piece.shape[1])
        copies.append(
            pltpu.make_async_copy(piece, panel_ref.at[pl.ds(lane * rows, rows), probes], panel_sem.at[n])
        )
    for copy in copies:
        copy.start()
    for step in range(steps):
        block_copy(blocks_ref, held_ref, sem, 0, LOCAL, step).start()
    for copy in copies:
        copy.wait()

    @pl.loop(0, steps)
    def _(step):
        block_copy(blocks_ref, held_ref, sem, 0, LOCAL, step).wait()
        for t in range(STEP):
            r = step * STEP + t
            total = None
            for j in range(0, LOCAL, 2):
                term = pair_dot(
                    [panel_ref[cols_ref[j + k, r]] for k in range(2)],
                    [held_ref[r, j + k] for k in range(2)],
                )
                total = term if total is None else total + term
            use(r, total)
        if done is not None:
            done(step)


def local_kernel(cols_ref, lane_ref, own_ref, prev_ref, across_ref, next_ref, blocks_ref, sum_ref, total_ref, total_sem, panel_ref, held_ref, panel_sem, sem):
    def use(r, total):
        total_ref[r] = total

    def done(step):
        at = pl.ds(step * STEP, STEP)
        pltpu.make_async_copy(total_ref.at[at], sum_ref.at[at], total_sem).start()

    pieces = (own_ref, prev_ref, across_ref, next_ref)
    local_products(lane_ref, pieces, blocks_ref, panel_ref, held_ref, panel_sem, sem, cols_ref, use, done)
    wait_all([sum_ref], total_sem)


def local_scratch(rows, part, size, kind):
    return [
        pltpu.VMEM((LANES * rows, part, size), kind),
        pltpu.VMEM((rows, LOCAL, size, size), kind),
        DMA((2 * LANES,)),
        DMA((rows // STEP,)),
    ]


def in_hbm(x):
    return pltpu.with_memory_space_constraint(x, pltpu.HBM)


def in_vmem(x):
    return pltpu.with_memory_space_constraint(x, pltpu.VMEM)


def local_part(cols, lane, pieces, blocks):
    rows, part, size = pieces[0].shape
    return pl.pallas_call(
        local_kernel,
        in_specs=[SMEM, SMEM] + [HBM] * 5,
        out_specs=HBM,
        scratch_shapes=[pltpu.VMEM((rows, part, size), jnp.float32), DMA] + local_scratch(rows, part, size, blocks.dtype),
        out_shape=pltpu.HBM((rows, part, size), jnp.float32),
        compiler_params=grant(24),
        name="local",
    )(cols, lane, *[in_hbm(x) for x in pieces], in_hbm(blocks))


def row_copies(blocks_ref, other_ref, far_ref, near_ref, far_sem, near_sem, probes, step):
    at = pl.ds(step * STEP, STEP)
    return (
        block_copy(blocks_ref, far_ref, far_sem, LOCAL, REMOTE, step),
        pltpu.make_async_copy(other_ref.at[at, probes], near_ref.at[at], near_sem.at[step]),
    )


def remote_products(fields, blocks_ref, other_ref, probes, far_ref, near_ref, far_sem, near_sem, use, ready=None):
    rows = near_ref.shape[0]
    steps = rows // STEP
    for step in range(steps):
        for copy in row_copies(blocks_ref, other_ref, far_ref, near_ref, far_sem, near_sem, probes, step):
            copy.start()
    if ready is not None:
        ready()

    @pl.loop(0, steps)
    def _(step):
        for copy in row_copies(blocks_ref, other_ref, far_ref, near_ref, far_sem, near_sem, probes, step):
            copy.wait()
        for t in range(STEP):
            r = step * STEP + t
            left = [
                jnp.concatenate([ref[refs[j, r]] for ref, refs in fields], axis=0) for j in range(REMOTE)
            ]
            use(r, pair_dot(left, [far_ref[r, j] for j in range(REMOTE)]), near_ref[r])


def remote_scratch(rows, part, size, kind, near_kind):
    return [
        pltpu.VMEM((rows, REMOTE, size, size), kind),
        pltpu.VMEM((rows, part, size), near_kind),
        DMA((rows // STEP,)),
        DMA((rows // STEP,)),
    ]


def slim_copies(got_refs, panel_ref, sem):
    count = got_refs[0].shape[0]
    return [
        pltpu.make_async_copy(ref, panel_ref.at[pl.ds(dz * count, count)], sem.at[dz]) for dz, ref in enumerate(got_refs)
    ]


def first_wide_kernel(refs_ref, table_ref, count_ref, got_ref, sum_ref, blocks_ref, own_ref, send_ref, src_ref, own_sem, send_sem, *scratch):
    rows, part, _ = own_ref.shape
    src_ref[rows] = jnp.zeros_like(src_ref[rows])

    def use(r, total, near):
        src_ref[r] = (near + total).astype(src_ref.dtype)

    remote_products([(got_ref, refs_ref)], blocks_ref, sum_ref, pl.ds(0, part), *scratch, use)
    start_wide(table_ref, count_ref, src_ref, send_ref, send_sem)
    own = pltpu.make_async_copy(src_ref.at[pl.ds(0, rows)], own_ref, own_sem)
    own.start()
    own.wait()
    wait_all([send_ref], send_sem)


def first_wide(refs, table, counts, got, sums, blocks, peers, slots):
    rows, _, size = sums.shape
    kind = got.dtype
    return pl.pallas_call(
        first_wide_kernel,
        in_specs=[SMEM, SMEM, SMEM, VMEM, HBM, HBM],
        out_specs=[HBM, HBM],
        scratch_shapes=[pltpu.VMEM((rows + 1, WIDE, size), kind), DMA, DMA]
        + remote_scratch(rows, WIDE, size, kind, sums.dtype),
        out_shape=[pltpu.HBM((rows, WIDE, size), kind), pltpu.HBM((peers, slots, WIDE, size), kind)],
        compiler_params=grant(24),
        name="first_wide",
    )(refs, table, counts, in_vmem(got), in_hbm(sums), in_hbm(blocks))


def first_slim_kernel(refs_ref, table_ref, count_ref, me_ref, *rest):
    got_refs, (sum_ref, blocks_ref, own_ref), rest = rest[:ZS], rest[ZS:ZS + 3], rest[ZS + 3:]
    turn_refs, (src_ref, panel_ref, own_sem, turn_sem, got_sem), scratch = rest[:PLANE], rest[PLANE:PLANE + 5], rest[PLANE + 5:]
    rows, part, _ = own_ref.shape
    src_ref[rows] = jnp.zeros_like(src_ref[rows])
    copies = slim_copies(got_refs, panel_ref, got_sem)
    for copy in copies:
        copy.start()

    def ready():
        for copy in copies:
            copy.wait()

    def use(r, total, near):
        src_ref[r] = (near + total).astype(src_ref.dtype)

    remote_products([(panel_ref, refs_ref)], blocks_ref, sum_ref, pl.ds(WIDE, part), *scratch, use, ready)
    start_slim(0, table_ref, count_ref, me_ref, src_ref, turn_refs, turn_sem)
    own = pltpu.make_async_copy(src_ref.at[pl.ds(0, rows)], own_ref, own_sem)
    own.start()
    own.wait()
    wait_all(turn_refs, turn_sem)


def first_slim(refs, table, counts, me, got, sums, blocks, peers, slots):
    rows, part, size = sums.shape
    slim, kind = part - WIDE, got[0].dtype
    return pl.pallas_call(
        first_slim_kernel,
        in_specs=[SMEM] * 4 + [HBM] * (ZS + 2),
        out_specs=[HBM] * (1 + PLANE),
        scratch_shapes=[
            pltpu.VMEM((rows + 1, slim, size), kind),
            pltpu.VMEM((peers * slots, slim, size), kind),
            DMA,
            DMA,
            DMA((ZS,)),
        ]
        + remote_scratch(rows, slim, size, kind, sums.dtype),
        out_shape=[pltpu.HBM((rows, slim, size), kind)] + slim_shapes(peers, slots, slim, size, kind),
        compiler_params=grant(24),
        name="first_slim",
    )(refs, table, counts, me, *[in_hbm(x) for x in got], in_hbm(sums), in_hbm(blocks))


def near_kernel(scale, cols_ref, lane_ref, *rest):
    pieces, rest = rest[:2 * LANES], rest[2 * LANES:]
    blocks_ref, probes_ref, near_ref, base_ref, panel_ref, held_ref, base_sem, panel_sem, sem = rest
    rows, _, size = base_ref.shape
    copy = pltpu.make_async_copy(probes_ref, base_ref, base_sem)
    copy.start()
    copy.wait()
    me = lane_ref[0]

    def use(r, total):
        base = base_ref[r].astype(jnp.float32)
        one = panel_ref[me * rows + r].astype(jnp.float32)
        at = pl.ds(pl.multiple_of(r * size, size), size)
        for k, other in enumerate((base, one, 2.0 * total - base)):
            value = jnp.sum(base * other, axis=0, keepdims=True)
            near_ref[k:k + 1, at] = value if scale[k] is None else value * scale[k]

    local_products(lane_ref, pieces, blocks_ref, panel_ref, held_ref, panel_sem, sem, cols_ref, use)


def near_part(cols, lane, pieces, blocks, base, scale):
    rows, part, size = base.shape
    panel, held, panel_sem, sem = local_scratch(rows, part, size, blocks.dtype)
    return pl.pallas_call(
        functools.partial(near_kernel, scale),
        in_specs=[SMEM, SMEM] + [HBM] * (2 * LANES + 2),
        out_specs=VMEM,
        scratch_shapes=[pltpu.VMEM(base.shape, base.dtype), panel, held, DMA, panel_sem, sem],
        out_shape=jax.ShapeDtypeStruct((3, rows * size), jnp.float32),
        compiler_params=grant(24),
        name="near",
    )(cols, lane, *[in_hbm(x) for x in pieces], in_hbm(blocks), in_hbm(base))


def moment_row(scale, near_ref, out_ref, size):
    out_ref[0:2] = near_ref[0:2]

    def use(r, total, base):
        at = pl.ds(pl.multiple_of(r * size, size), size)
        value = near_ref[2:3, at] + 2.0 * jnp.sum(total * base.astype(jnp.float32), axis=0, keepdims=True)
        out_ref[2:3, at] = value if scale is None else value * scale

    return use


def wide_kernel(refs_ref, wide_ref, near_ref, base_ref, blocks_ref, out_ref, *scratch):
    use = moment_row(None, near_ref, out_ref, base_ref.shape[2])
    remote_products([(wide_ref, refs_ref)], blocks_ref, base_ref, pl.ds(0, WIDE), *scratch, use)


def wide_part(refs, wide, near, base, blocks):
    rows, _, size = base.shape
    return pl.pallas_call(
        wide_kernel,
        in_specs=[SMEM, VMEM, VMEM, HBM, HBM],
        out_specs=VMEM,
        scratch_shapes=remote_scratch(rows, WIDE, size, blocks.dtype, base.dtype),
        out_shape=jax.ShapeDtypeStruct(near.shape, near.dtype),
        compiler_params=grant(24),
        name="wide",
    )(refs, in_vmem(wide), near, in_hbm(base), in_hbm(blocks))


def moments_kernel(scale, refs_ref, *rest):
    got_refs, (near_ref, base_ref, blocks_ref, out_ref, panel_ref, got_sem), scratch = rest[:ZS], rest[ZS:ZS + 6], rest[ZS + 6:]
    copies = slim_copies(got_refs, panel_ref, got_sem)
    for copy in copies:
        copy.start()
    _, part, size = base_ref.shape

    def ready():
        for copy in copies:
            copy.wait()

    use = moment_row(scale, near_ref, out_ref, size)
    remote_products([(panel_ref, refs_ref)], blocks_ref, base_ref, pl.ds(WIDE, part - WIDE), *scratch, use, ready)


def moments_part(refs, got, near, base, blocks, scale):
    rows, part, size = base.shape
    slim = part - WIDE
    return pl.pallas_call(
        functools.partial(moments_kernel, scale),
        in_specs=[SMEM] + [HBM] * ZS + [VMEM, HBM, HBM],
        out_specs=VMEM,
        scratch_shapes=[pltpu.VMEM((ZS * got[0].shape[0], slim, size), base.dtype), DMA((ZS,))]
        + remote_scratch(rows, slim, size, blocks.dtype, base.dtype),
        out_shape=jax.ShapeDtypeStruct(near.shape, near.dtype),
        compiler_params=grant(24),
        name="moments",
    )(refs, *[in_hbm(x) for x in got], near, in_hbm(base), in_hbm(blocks))


def plane_step(i, k):
    z, x, core = i // PLANE, i // CS % XS, i % CS
    return z * PLANE + (x + k // CS) % XS * CS + (core + k) % CS


def across_plane(sends):
    size = ZS * PLANE
    return [sends[0]] + [
        lax.ppermute(sends[k], "dom", [(i, plane_step(i, k)) for i in range(size)]) for k in range(1, PLANE)
    ]


def along_z(sends, steps):
    size = ZS * PLANE
    return {dz: lax.ppermute(sends[dz], "dom", [(i, (i + dz * PLANE) % size) for i in range(size)]) for dz in steps}


def slim_kernel(me_ref, refs_ref, out_ref, *, slots):
    me = me_ref[0]
    refs = refs_ref[...]
    e = refs // slots
    dz = (me // PLANE - e // PLANE) & (ZS - 1)
    dx = (me // CS - e // CS) & (XS - 1)
    core = (me - e) & (CS - 1)
    out_ref[...] = (dz * PLANE + dx * CS + core) * slots + refs - e * slots


def slim_slots(refs, slots, me):
    return pl.pallas_call(
        functools.partial(slim_kernel, slots=slots),
        in_specs=[SMEM, VMEM],
        out_specs=VMEM,
        out_shape=jax.ShapeDtypeStruct(refs.shape, refs.dtype),
        compiler_params=grant(62),
        name="slim_slots",
    )(me, refs)


def on_device(blocks, local_cols, remote_refs, send_blocks, send_counts, probes):
    rows, _, size, _ = blocks.shape
    peers, slots = send_blocks.shape[2], send_blocks.shape[3]
    table = send_blocks.transpose(0, 3, 1, 2)[0]
    counts = send_counts[0, 0]
    cols = local_cols.T
    refs = remote_refs.T
    lane = lax.axis_index("grp").astype(jnp.int32).reshape(1)
    me = lax.axis_index("dom").astype(jnp.int32).reshape(1)
    norm = 1.0 / math.sqrt(PROBES)
    scale = (
        jackson(0, KMOM) * norm,
        2.0 * jackson(1, KMOM) * norm,
        2.0 * jackson(2, KMOM) * norm,
    )

    def exchange(send):
        got = lax.all_to_all(send, "dom", split_axis=0, concat_axis=0, tiled=True)
        return got.reshape(peers * slots, send.shape[2], size)

    def panel(own):
        pieces = [own]
        for shift in (1, 2, 3):
            pieces.append(lax.ppermute(own, "grp", [(i, (i + shift) % LANES) for i in range(LANES)]))
        return pieces

    send = pack_wide(table, counts, probes, peers, slots, rows, size)
    wide = exchange(send)
    base, *sides = pack_slim(table, counts, me, probes, peers, slots, rows, size)
    sides = across_plane(sides)
    pieces = panel(base)
    sides = turn(sides, base)
    slim = {0: sides[0]} | along_z(sides, EARLY)
    sums = local_part(cols, lane, pieces, blocks)
    slim |= along_z(sides, LATE)
    slim = [slim[dz] for dz in range(ZS)]
    slim_refs = slim_slots(refs, slots, me)
    first, send = first_wide(refs, table, counts, wide, sums, blocks, peers, slots)
    wide = exchange(send)
    pieces = panel(first)
    slim_first, *sides = first_slim(slim_refs, table, counts, me, slim, sums, blocks, peers, slots)
    sides = across_plane(sides)
    pieces = pieces + panel(slim_first)
    sides = turn(sides, slim_first)
    slim = {0: sides[0]} | along_z(sides, (4, 3, 5, 2, 6, 1, 7))
    slim = [slim[dz] for dz in range(ZS)]
    near = near_part(cols, lane, pieces, blocks, base, scale[:2] + (None,))
    near = wide_part(refs, wide, near, base, blocks)
    return moments_part(slim_refs, slim, near, base, blocks, scale[2])


def solution(mesh):
    in_specs = (
        P(("dom", "grp"), None, None, None),
        P(("dom", "grp"), None),
        P(("dom", "grp"), None),
        P("dom", "grp", None, None),
        P("dom", "grp", None),
        P(None, ("dom", "grp")),
    )
    out_specs = P(None, ("dom", "grp"))

    return jax.shard_map(on_device, mesh=mesh, in_specs=in_specs, out_specs=out_specs, check_vma=False)
```

time: 178 us -> 240 us (1.35); the launches traced: 178 us -> 237 us
  starting transfers between devices: 24.1 us -> 64.1 us
  Pallas kernels: 28.5 us -> 48.6 us
  waiting for transfers between devices: 123 us -> 119 us
    ppermute x0 -> x28, waiting for transfers between devices: none -> 66.6 us  [the longest x14 44.4 us: along_z(): lax.ppermute(sends[dz], 'dom', [(i, (i + dz * PLANE) % size) for i in ran...]
    all_to_all x2, waiting for transfers between devices: 53.3 us -> 6.68 us  [exchange(): got = lax.all_to_all(send, 'dom', split_axis=0, concat_axis=0, tiled=True)]
    ppermute x0 -> x28, starting transfers between devices: none -> 37.5 us  [the longest x14 23.4 us: along_z(): lax.ppermute(sends[dz], 'dom', [(i, (i + dz * PLANE) % size) for i in ran...]
    ppermute x6 -> x9, waiting for transfers between devices: 69.9 us -> 46 us  [panel(): lax.ppermute(own, 'grp', [(i, (i + shift) % LANES) for i in range(LANES)])]
    pallas_call x4 -> x10, Pallas kernels: 21.3 us -> 40.7 us  [the longest x1 8.09 us: near_part(): pl.pallas_call(functools.partial(near_kernel, scale), in_specs=[SMEM, SME...]
    ppermute x6 -> x9, starting transfers between devices: 6.86 us -> 8.8 us  [panel(): lax.ppermute(own, 'grp', [(i, (i + shift) % LANES) for i in range(LANES)])]
  transfers between devices with their start and end apart: 8 -> 39, of which waited for: 8 -> 20; matrix products, arithmetic and copies ran while one was open for 0% -> 0% of each run, Pallas kernels for 9% -> 15%
where the time goes in v2:
time: 240 us; the launch traced here: 237 us
  waiting for transfers between devices  119 us (50%)
  starting transfers between devices  64.1 us (27%)
  Pallas kernels  48.6 us (20%)
  local copies, waits for them, and re-layouts  4.34 us (2%)
    ppermute x9, waiting for transfers between devices, panel(): lax.ppermute(own, 'grp', [(i, (i + shift) % LANES) for i in range(LANES)])  46 us
    ppermute x14, waiting for transfers between devices, along_z(): lax.ppermute(sends[dz], 'dom', [(i, (i + dz * PLANE) % size) for i in ran...  44.4 us
    ppermute x14, starting transfers between devices, along_z(): lax.ppermute(sends[dz], 'dom', [(i, (i + dz * PLANE) % size) for i in ran...  23.4 us
    ppermute x14, waiting for transfers between devices, across_plane(): lax.ppermute(sends[k], 'dom', [(i, plane_step(i, k)) for i in range(size)])  22.2 us
    all_to_all x2, starting transfers between devices, exchange(): got = lax.all_to_all(send, 'dom', split_axis=0, concat_axis=0, tiled=True)  17.9 us
    ppermute x14, starting transfers between devices, across_plane(): lax.ppermute(sends[k], 'dom', [(i, plane_step(i, k)) for i in range(size)])  14.1 us
    ppermute x9, starting transfers between devices, panel(): lax.ppermute(own, 'grp', [(i, (i + shift) % LANES) for i in range(LANES)])  8.8 us
    pallas_call x1, Pallas kernels, near_part(): pl.pallas_call(functools.partial(near_kernel, scale), in_specs=[SMEM, SME...  8.09 us
  transfers between devices with their start and end apart: 39, of which 20 were waited for; matrix products, arithmetic and copies ran while one was open for 0% of the time, Pallas kernels for 15%

profile of v2, /device:TPU:16, one launch (start us, length us, event | category | flops | bytes accessed | tf_op | source)
XLA Modules:
  0.0 237.0 jit_solution(12092977537017377478)
XLA Ops:
  0.0 2.7 %pack_wide.1 = bf16[64,3,48,128]{3,2,1,0:T(8,128)(2,1)} custom-call(s32[3,1,64]{2,1,0:T(1,128)} %bitcast.10, s32[64]{0:T(128)} %bitcast.19, bf16[64,6144]{1,0:T(8,128)(2,1)} %probes_ref.3), custom_call_target="tpu_custom_call" | custom-call | tf_op jit(solution)/shard_map/pack_wide/pallas_call | solution.py:102
  2.7 12.2 %all-to-all-start = ((bf16[64,3,48,128]{3,2,1,0:T(8,128)(2,1)}), bf16[64,3,48,128]{3,2,1,0:T(8,128)(2,1)}, u32[]{:S(2)}, u32[]{:S(2)}) async-start(bf16[64,3,48,128]{3,2,1,0:T(8,128)(2,1)} %pack_wide.1), calls=%async_computation | async-start | bytes 4718592 | tf_op jit(solution)/shard_map/all_to_all | solution.py:521
  14.9 2.9 %pack_slim.1 = (bf16[48,64,128]{2,1,0:T(8,128)(2,1)}, bf16[24,16,128]{2,1,0:T(8,128)(2,1)}, bf16[24,16,128]{2,1,0:T(8,128)(2,1)}, bf16[24,16,128]{2,1,0:T(8,128)...) custom-call(s32[3,1,64]{2,1,0:T(1,128)} %bitcast.11, ...), custom_call_target="tpu_custom_call" | custom-call | tf_op jit(solution)/shard_map/pack_slim/pallas_call | solution.py:131
  20.8 33.5 %collective-permute-done.14.prev_ref = bf16[48,64,128]{2,1,0:T(8,128)(2,1)S(1)} collective-permute-done((bf16[48,64,128]{2,1,0:T(8,128)(2,1)}, bf16[48,64,128]{2,1,0:T(8,128)(2,1)S(1)}, u32[]{:S(2)}, u32[]{:S(2)}) %collective-permute-start.14) | collective-permute-done | bytes 786464 | tf_op jit(solution)/shard_map/ppermute | solution.py:527
  57.1 7.9 %local.1.rest_8_.sum_ref = f32[48,64,128]{2,1,0:T(8,128)} custom-call(s32[4,48]{1,0:T(4,128)S(1)} %bitcast.17, s32[1]{0:T(128)} %bitcast.7.lane_ref, bf16[48,64,128]{2,1,0:T(8,128)(2,1)} %get-tuple-element.49.refs_8_.own_ref.rest_9_.base_ref, bf16[48,64,128]{2,1,0:T(8,128)(2,1)} %copy-done.7, bf16[48,64,128]{2,1,0:T(8,128)(2,1)} %copy-done.8, ...), custom_call_target="tpu_custom_call" | custom-call | tf_op jit(solution)/shard_map/local/pallas_call | solution.py:242
  65.0 6.7 %all-to-all-done = bf16[64,3,48,128]{3,2,1,0:T(8,128)(2,1)} async-done(((bf16[64,3,48,128]{3,2,1,0:T(8,128)(2,1)}), bf16[64,3,48,128]{3,2,1,0:T(8,128)(2,1)}, u32[]{:S(2)}, u32[]{:S(2)}) %all-to-all-start) | async-done | bytes 2359328 | tf_op jit(solution)/shard_map/all_to_all | solution.py:521
  71.7 6.4 %first_wide.1 = (bf16[48,48,128]{2,1,0:T(8,128)(2,1)}, bf16[64,3,48,128]{3,2,1,0:T(8,128)(2,1)}) custom-call(s32[2,48]{1,0:T(2,128)S(1)} %bitcast.15, s32[3,1,64]{2,1,0:T(1,128)S(1)} %bitcast.12, s32[64]{0:T(128)S(1)} %bitcast.21, bf16[192,48,128]{2,1,0:T(8,128)(2,1)} %bitcast.8.got_ref, f32[48,64,128]{2,1,0:T(8,128)} %local.1.rest_8_.sum_ref, ...), custom_call_target="tpu_custom_call" | custom-call | tf_op jit(solution)/shard_map/first_wide/pallas_call | solution.py:316
  78.2 5.7 %all-to-all-start.1 = ((bf16[64,3,48,128]{3,2,1,0:T(8,128)(2,1)}), bf16[64,3,48,128]{3,2,1,0:T(8,128)(2,1)}, u32[]{:S(2)}, u32[]{:S(2)}) async-start(bf16[64,3,48,128]{3,2,1,0:T(8,128)(2,1)} %get-tuple-element.75), calls=%async_computation.1 | async-start | bytes 4718592 | tf_op jit(solution)/shard_map/all_to_all | solution.py:521
  91.9 3.2 %collective-permute-done.1.refs_2_ = bf16[24,16,128]{2,1,0:T(8,128)(2,1)S(1)} collective-permute-done((bf16[24,16,128]{2,1,0:T(8,128)(2,1)S(1)}, bf16[24,16,128]{2,1,0:T(8,128)(2,1)S(1)}, u32[]{:S(2)}, u32[]{:S(2)}) %collective-permute-start.1) | collective-permute-done | bytes 98336 | tf_op jit(solution)/shard_map/ppermute | solution.py:474
  95.1 2.9 %collective-permute-done.2.refs_3_ = bf16[24,16,128]{2,1,0:T(8,128)(2,1)S(1)} collective-permute-done((bf16[24,16,128]{2,1,0:T(8,128)(2,1)S(1)}, bf16[24,16,128]{2,1,0:T(8,128)(2,1)S(1)}, u32[]{:S(2)}, u32[]{:S(2)}) %collective-permute-start.2) | collective-permute-done | bytes 98336 | tf_op jit(solution)/shard_map/ppermute | solution.py:474
  98.0 6.0 %collective-permute-done.3.refs_4_ = bf16[24,16,128]{2,1,0:T(8,128)(2,1)S(1)} collective-permute-done((bf16[24,16,128]{2,1,0:T(8,128)(2,1)S(1)}, bf16[24,16,128]{2,1,0:T(8,128)(2,1)S(1)}, u32[]{:S(2)}, u32[]{:S(2)}) %collective-permute-start.3) | collective-permute-done | bytes 98336 | tf_op jit(solution)/shard_map/ppermute | solution.py:474
  108.4 3.5 %collective-permute-start.7 = (bf16[24,16,128]{2,1,0:T(8,128)(2,1)}, bf16[24,16,128]{2,1,0:T(8,128)(2,1)S(1)}, u32[]{:S(2)}, u32[]{:S(2)}) collective-permute-start(bf16[24,16,128]{2,1,0:T(8,128)(2,1)} %get-tuple-element.51), channel_id=1, source_target_pairs={{0,32},{4,36},{8,40},{12,44},{16,48},{20,52},{24,56},{28,60},{32,6... | collective-permute-start | bytes 294920 | tf_op jit(solution)/shard_map/ppermute | solution.py:480
  113.7 3.9 %collective-permute-start.9 = (bf16[24,16,128]{2,1,0:T(8,128)(2,1)}, bf16[24,16,128]{2,1,0:T(8,128)(2,1)S(1)}, u32[]{:S(2)}, u32[]{:S(2)}) collective-permute-start(bf16[24,16,128]{2,1,0:T(8,128)(2,1)} %get-tuple-element.53), channel_id=1, source_target_pairs={{0,96},{4,100},{8,104},{12,108},{16,112},{20,116},{24,120},{28,124... | collective-permute-start | bytes 294920 | tf_op jit(solution)/shard_map/ppermute | solution.py:480
  117.7 2.2 collective-permute-start.10
  119.8 2.8 %collective-permute-start.11 = (bf16[24,16,128]{2,1,0:T(8,128)(2,1)}, bf16[24,16,128]{2,1,0:T(8,128)(2,1)S(1)}, u32[]{:S(2)}, u32[]{:S(2)}) collective-permute-start(bf16[24,16,128]{2,1,0:T(8,128)(2,1)} %get-tuple-element.55), channel_id=1, source_target_pairs={{0,160},{4,164},{8,168},{12,172},{16,176},{20,180},{24,184},{28,18... | collective-permute-start | bytes 294920 | tf_op jit(solution)/shard_map/ppermute | solution.py:480
  122.7 18.4 %collective-permute-done.7.rest_1_ = bf16[24,16,128]{2,1,0:T(8,128)(2,1)S(1)} collective-permute-done((bf16[24,16,128]{2,1,0:T(8,128)(2,1)}, bf16[24,16,128]{2,1,0:T(8,128)(2,1)S(1)}, u32[]{:S(2)}, u32[]{:S(2)}) %collective-permute-start.7) | collective-permute-done | bytes 98336 | tf_op jit(solution)/shard_map/ppermute | solution.py:480
  141.0 2.1 collective-permute-start.12
  143.2 3.5 %collective-permute-done.8.rest_2_ = bf16[24,16,128]{2,1,0:T(8,128)(2,1)S(1)} collective-permute-done((bf16[24,16,128]{2,1,0:T(8,128)(2,1)}, bf16[24,16,128]{2,1,0:T(8,128)(2,1)S(1)}, u32[]{:S(2)}, u32[]{:S(2)}) %collective-permute-start.8) | collective-permute-done | bytes 98336 | tf_op jit(solution)/shard_map/ppermute | solution.py:480
  148.1 5.4 %collective-permute-done.9.rest_3_ = bf16[24,16,128]{2,1,0:T(8,128)(2,1)S(1)} collective-permute-done((bf16[24,16,128]{2,1,0:T(8,128)(2,1)}, bf16[24,16,128]{2,1,0:T(8,128)(2,1)S(1)}, u32[]{:S(2)}, u32[]{:S(2)}) %collective-permute-start.9) | collective-permute-done | bytes 98336 | tf_op jit(solution)/shard_map/ppermute | solution.py:480
  153.5 4.0 %collective-permute-done.10.rest_4_ = bf16[24,16,128]{2,1,0:T(8,128)(2,1)S(1)} collective-permute-done((bf16[24,16,128]{2,1,0:T(8,128)(2,1)}, bf16[24,16,128]{2,1,0:T(8,128)(2,1)S(1)}, u32[]{:S(2)}, u32[]{:S(2)}) %collective-permute-start.10) | collective-permute-done | bytes 98336 | tf_op jit(solution)/shard_map/ppermute | solution.py:480
  158.9 5.8 %first_slim.1 = (bf16[48,16,128]{2,1,0:T(8,128)(2,1)}, bf16[24,16,128]{2,1,0:T(8,128)(2,1)}, bf16[24,16,128]{2,1,0:T(8,128)(2,1)}, bf16[24,16,128]{2,1,0:T(8,128...) custom-call(s32[2,48]{1,0:T(2,128)S(1)} %copy-done.3, ...), custom_call_target="tpu_custom_call" | custom-call | tf_op jit(solution)/shard_map/first_slim/pallas_call | solution.py:355
  174.7 2.4 %collective-permute-done.20.refs_4_ = bf16[24,16,128]{2,1,0:T(8,128)(2,1)S(1)} collective-permute-done((bf16[24,16,128]{2,1,0:T(8,128)(2,1)}, bf16[24,16,128]{2,1,0:T(8,128)(2,1)S(1)}, u32[]{:S(2)}, u32[]{:S(2)}) %collective-permute-start.20) | collective-permute-done | bytes 98336 | tf_op jit(solution)/shard_map/ppermute | solution.py:474
  178.2 5.4 %collective-permute-done.22.refs_6_ = bf16[24,16,128]{2,1,0:T(8,128)(2,1)} collective-permute-done((bf16[24,16,128]{2,1,0:T(8,128)(2,1)}, bf16[24,16,128]{2,1,0:T(8,128)(2,1)}, u32[]{:S(2)}, u32[]{:S(2)}) %collective-permute-start.22) | collective-permute-done | bytes 98336 | tf_op jit(solution)/shard_map/ppermute | solution.py:474
  187.1 5.6 %collective-permute-done.24.rest_1_ = bf16[24,16,128]{2,1,0:T(8,128)(2,1)S(1)} collective-permute-done((bf16[24,16,128]{2,1,0:T(8,128)(2,1)}, bf16[24,16,128]{2,1,0:T(8,128)(2,1)S(1)}, u32[]{:S(2)}, u32[]{:S(2)}) %collective-permute-start.24) | collective-permute-done | bytes 98336 | tf_op jit(solution)/shard_map/ppermute | solution.py:480
  192.7 7.4 %collective-permute-done.25.rest_2_ = bf16[24,16,128]{2,1,0:T(8,128)(2,1)S(1)} collective-permute-done((bf16[24,16,128]{2,1,0:T(8,128)(2,1)}, bf16[24,16,128]{2,1,0:T(8,128)(2,1)S(1)}, u32[]{:S(2)}, u32[]{:S(2)}) %collective-permute-start.25) | collective-permute-done | bytes 98336 | tf_op jit(solution)/shard_map/ppermute | solution.py:480
  200.3 3.1 %collective-permute-done.34.rest_5_ = bf16[48,16,128]{2,1,0:T(8,128)(2,1)S(1)} collective-permute-done((bf16[48,16,128]{2,1,0:T(8,128)(2,1)}, bf16[48,16,128]{2,1,0:T(8,128)(2,1)S(1)}, u32[]{:S(2)}, u32[]{:S(2)}) %collective-permute-start.34) | collective-permute-done | bytes 196640 | tf_op jit(solution)/shard_map/ppermute | solution.py:527
  203.9 4.3 %collective-permute-done.35.rest_6_ = bf16[48,16,128]{2,1,0:T(8,128)(2,1)S(1)} collective-permute-done((bf16[48,16,128]{2,1,0:T(8,128)(2,1)}, bf16[48,16,128]{2,1,0:T(8,128)(2,1)S(1)}, u32[]{:S(2)}, u32[]{:S(2)}) %collective-permute-start.35) | collective-permute-done | bytes 196640 | tf_op jit(solution)/shard_map/ppermute | solution.py:527
  208.2 3.2 %collective-permute-done.36.rest_7_ = bf16[48,16,128]{2,1,0:T(8,128)(2,1)S(1)} collective-permute-done((bf16[48,16,128]{2,1,0:T(8,128)(2,1)}, bf16[48,16,128]{2,1,0:T(8,128)(2,1)S(1)}, u32[]{:S(2)}, u32[]{:S(2)}) %collective-permute-start.36) | collective-permute-done | bytes 196640 | tf_op jit(solution)/shard_map/ppermute | solution.py:527
  211.4 2.7 %collective-permute-start.27 = (bf16[24,16,128]{2,1,0:T(8,128)(2,1)}, bf16[24,16,128]{2,1,0:T(8,128)(2,1)S(1)}, u32[]{:S(2)}, u32[]{:S(2)}) collective-permute-start(bf16[24,16,128]{2,1,0:T(8,128)(2,1)} %get-tuple-element.71), channel_id=1, source_target_pairs={{0,128},{4,132},{8,136},{12,140},{16,144},{20,148},{24,152},{28,15... | collective-permute-start | bytes 294920 | tf_op jit(solution)/shard_map/ppermute | solution.py:480
  218.2 8.1 %near.1.near_ref = f32[3,6144]{1,0:T(4,128)S(1)} custom-call(s32[4,48]{1,0:T(4,128)S(1)} %bitcast.18, s32[1]{0:T(128)} %bitcast.7.lane_ref, bf16[48,48,128]{2,1,0:T(8,128)(2,1)} %get-tuple-element.76.rest_0_, bf16[48,48,128]{2,1,0:T(8,128)(2,1)} %copy-done.11, bf16[48,48,128]{2,1,0:T(8,128)(2,1)} %copy-done.12, ...), custom_call_target="tpu_custom_call" | custom-call | tf_op jit(solution)/shard_map/near/pallas_call | solution.py:396
  226.4 4.7 %wide.1.rest_8_ = f32[3,6144]{1,0:T(4,128)S(1)} custom-call(s32[2,48]{1,0:T(2,128)S(1)} %bitcast.16, bf16[192,48,128]{2,1,0:T(8,128)(2,1)} %bitcast.9.wide_ref, f32[3,6144]{1,0:T(4,128)S(1)} %near.1.near_ref, bf16[48,64,128]{2,1,0:T(8,128)(2,1)} %get-tuple-element.49.refs_8_.own_ref.rest_9_.base_ref, bf16[48,6,128,128]{3,2,1,0:T(8,128)(2,1)} %rest_10_.1), custom_call_target="tpu_custom_call" | custom-call | tf_op jit(solution)/shard_map/wide/pallas_call | solution.py:425
  231.9 5.0 %moments.1 = f32[3,6144]{1,0:T(4,128)} custom-call(s32[2,48]{1,0:T(2,128)S(1)} %copy-done.4, bf16[24,16,128]{2,1,0:T(8,128)(2,1)} %get-tuple-element.67.rest_0_, bf16[24,16,128]{2,1,0:T(8,128)(2,1)} %copy-done.16, bf16[24,16,128]{2,1,0:T(8,128)(2,1)} %copy-done.17, bf16[24,16,128]{2,1,0:T(8,128)(2,1)} %copy-done.18, bf16[24,16,128]{2,1,0:T(8,128)(2,1)} %copy-done.20, ...), custom_call_target="tpu_custom_call" | custom-call | tf_op jit(solution)/shard_map/moments/pallas_call | solution.py:454
  (153 shorter events, 42.8 us)
Async XLA Ops:
  2.7 69.0 %all-to-all-start = ((bf16[64,3,48,128]{3,2,1,0:T(8,128)(2,1)}), bf16[64,3,48,128]{3,2,1,0:T(8,128)(2,1)}, u32[]{:S(2)}, u32[]{:S(2)}) async-start(bf16[64,3,48,128]{3,2,1,0:T(8,128)(2,1)} %pack_wide.1), calls=%async_computation | async-start | bytes 4718592 | tf_op jit(solution)/shard_map/all_to_all | solution.py:521
  17.8 36.6 %collective-permute-start.14 = (bf16[48,64,128]{2,1,0:T(8,128)(2,1)}, bf16[48,64,128]{2,1,0:T(8,128)(2,1)S(1)}, u32[]{:S(2)}, u32[]{:S(2)}) collective-permute-start(bf16[48,64,128]{2,1,0:T(8,128)(2,1)} %get-tuple-element.49.refs_8_.own_ref.rest_9_.base_ref), channel_id=1, source_target_pairs={{0,1},{1,2},{2,3},{3,0},{4,5},{5,6},{6,7},{7,4},{8,9},{9,10},{10,1... | collective-permute-start | bytes 2359304 | tf_op jit(solution)/shard_map/ppermute | solution.py:527
  19.1 35.2 %collective-permute-start.15 = (bf16[48,64,128]{2,1,0:T(8,128)(2,1)}, bf16[48,64,128]{2,1,0:T(8,128)(2,1)S(1)}, u32[]{:S(2)}, u32[]{:S(2)}) collective-permute-start(bf16[48,64,128]{2,1,0:T(8,128)(2,1)} %get-tuple-element.49.refs_8_.own_ref.rest_9_.base_ref), channel_id=1, source_target_pairs={{0,2},{1,3},{2,0},{3,1},{4,6},{5,7},{6,4},{7,5},{8,10},{9,11},{10,... | collective-permute-start | bytes 2359304 | tf_op jit(solution)/shard_map/ppermute | solution.py:527
  19.8 36.4 %collective-permute-start.16 = (bf16[48,64,128]{2,1,0:T(8,128)(2,1)}, bf16[48,64,128]{2,1,0:T(8,128)(2,1)S(1)}, u32[]{:S(2)}, u32[]{:S(2)}) collective-permute-start(bf16[48,64,128]{2,1,0:T(8,128)(2,1)} %get-tuple-element.49.refs_8_.own_ref.rest_9_.base_ref), channel_id=1, source_target_pairs={{0,3},{1,0},{2,1},{3,2},{4,7},{5,4},{6,5},{7,6},{8,11},{9,8},{10,9... | collective-permute-start | bytes 2359304 | tf_op jit(solution)/shard_map/ppermute | solution.py:527
  78.2 148.1 %all-to-all-start.1 = ((bf16[64,3,48,128]{3,2,1,0:T(8,128)(2,1)}), bf16[64,3,48,128]{3,2,1,0:T(8,128)(2,1)}, u32[]{:S(2)}, u32[]{:S(2)}) async-start(bf16[64,3,48,128]{3,2,1,0:T(8,128)(2,1)} %get-tuple-element.75), calls=%async_computation.1 | async-start | bytes 4718592 | tf_op jit(solution)/shard_map/all_to_all | solution.py:521
  84.0 11.1 %collective-permute-start.1 = (bf16[24,16,128]{2,1,0:T(8,128)(2,1)S(1)}, bf16[24,16,128]{2,1,0:T(8,128)(2,1)S(1)}, u32[]{:S(2)}, u32[]{:S(2)}) collective-permute-start(bf16[24,16,128]{2,1,0:T(8,128)(2,1)S(1)} %copy-done.46), channel_id=1, source_target_pairs={{0,8},{4,12},{8,16},{12,20},{16,24},{20,28},{24,0},{28,4},{32,40},... | collective-permute-start | bytes 294920 | tf_op jit(solution)/shard_map/ppermute | solution.py:474
  85.6 12.4 %collective-permute-start.2 = (bf16[24,16,128]{2,1,0:T(8,128)(2,1)S(1)}, bf16[24,16,128]{2,1,0:T(8,128)(2,1)S(1)}, u32[]{:S(2)}, u32[]{:S(2)}) collective-permute-start(bf16[24,16,128]{2,1,0:T(8,128)(2,1)S(1)} %copy-done.45), channel_id=1, source_target_pairs={{0,12},{4,8},{8,20},{12,16},{16,28},{20,24},{24,4},{28,0},{32,44},... | collective-permute-start | bytes 294920 | tf_op jit(solution)/shard_map/ppermute | solution.py:474
  86.8 17.2 %collective-permute-start.3 = (bf16[24,16,128]{2,1,0:T(8,128)(2,1)S(1)}, bf16[24,16,128]{2,1,0:T(8,128)(2,1)S(1)}, u32[]{:S(2)}, u32[]{:S(2)}) collective-permute-start(bf16[24,16,128]{2,1,0:T(8,128)(2,1)S(1)} %copy-done.44), channel_id=1, source_target_pairs={{0,16},{4,20},{8,24},{12,28},{16,0},{20,4},{24,8},{28,12},{32,48},... | collective-permute-start | bytes 294920 | tf_op jit(solution)/shard_map/ppermute | solution.py:474
  88.6 17.2 %collective-permute-start.4 = (bf16[24,16,128]{2,1,0:T(8,128)(2,1)S(1)}, bf16[24,16,128]{2,1,0:T(8,128)(2,1)S(1)}, u32[]{:S(2)}, u32[]{:S(2)}) collective-permute-start(bf16[24,16,128]{2,1,0:T(8,128)(2,1)S(1)} %copy-done.43), channel_id=1, source_target_pairs={{0,20},{4,16},{8,28},{12,24},{16,4},{20,0},{24,12},{28,8},{32,52},... | collective-permute-start | bytes 294920 | tf_op jit(solution)/shard_map/ppermute | solution.py:474
  90.1 15.7 %collective-permute-start.5 = (bf16[24,16,128]{2,1,0:T(8,128)(2,1)S(1)}, bf16[24,16,128]{2,1,0:T(8,128)(2,1)S(1)}, u32[]{:S(2)}, u32[]{:S(2)}) collective-permute-start(bf16[24,16,128]{2,1,0:T(8,128)(2,1)S(1)} %copy-done.42), channel_id=1, source_target_pairs={{0,24},{4,28},{8,0},{12,4},{16,8},{20,12},{24,16},{28,20},{32,56},... | collective-permute-start | bytes 294920 | tf_op jit(solution)/shard_map/ppermute | solution.py:474
  95.1 10.7 %collective-permute-start.6 = (bf16[24,16,128]{2,1,0:T(8,128)(2,1)S(1)}, bf16[24,16,128]{2,1,0:T(8,128)(2,1)S(1)}, u32[]{:S(2)}, u32[]{:S(2)}) collective-permute-start(bf16[24,16,128]{2,1,0:T(8,128)(2,1)S(1)} %copy-done.41), channel_id=1, source_target_pairs={{0,28},{4,24},{8,4},{12,0},{16,12},{20,8},{24,20},{28,16},{32,60},... | collective-permute-start | bytes 294920 | tf_op jit(solution)/shard_map/ppermute | solution.py:474
  108.4 32.6 %collective-permute-start.7 = (bf16[24,16,128]{2,1,0:T(8,128)(2,1)}, bf16[24,16,128]{2,1,0:T(8,128)(2,1)S(1)}, u32[]{:S(2)}, u32[]{:S(2)}) collective-permute-start(bf16[24,16,128]{2,1,0:T(8,128)(2,1)} %get-tuple-element.51), channel_id=1, source_target_pairs={{0,32},{4,36},{8,40},{12,44},{16,48},{20,52},{24,56},{28,60},{32,6... | collective-permute-start | bytes 294920 | tf_op jit(solution)/shard_map/ppermute | solution.py:480
  111.9 34.8 %collective-permute-start.8 = (bf16[24,16,128]{2,1,0:T(8,128)(2,1)}, bf16[24,16,128]{2,1,0:T(8,128)(2,1)S(1)}, u32[]{:S(2)}, u32[]{:S(2)}) collective-permute-start(bf16[24,16,128]{2,1,0:T(8,128)(2,1)} %get-tuple-element.52), channel_id=1, source_target_pairs={{0,64},{4,68},{8,72},{12,76},{16,80},{20,84},{24,88},{28,92},{32,9... | collective-permute-start | bytes 294920 | tf_op jit(solution)/shard_map/ppermute | solution.py:480
  113.7 39.8 %collective-permute-start.9 = (bf16[24,16,128]{2,1,0:T(8,128)(2,1)}, bf16[24,16,128]{2,1,0:T(8,128)(2,1)S(1)}, u32[]{:S(2)}, u32[]{:S(2)}) collective-permute-start(bf16[24,16,128]{2,1,0:T(8,128)(2,1)} %get-tuple-element.53), channel_id=1, source_target_pairs={{0,96},{4,100},{8,104},{12,108},{16,112},{20,116},{24,120},{28,124... | collective-permute-start | bytes 294920 | tf_op jit(solution)/shard_map/ppermute | solution.py:480
  117.7 39.8 %collective-permute-start.10 = (bf16[24,16,128]{2,1,0:T(8,128)(2,1)}, bf16[24,16,128]{2,1,0:T(8,128)(2,1)S(1)}, u32[]{:S(2)}, u32[]{:S(2)}) collective-permute-start(bf16[24,16,128]{2,1,0:T(8,128)(2,1)} %get-tuple-element.54), channel_id=1, source_target_pairs={{0,128},{4,132},{8,136},{12,140},{16,144},{20,148},{24,152},{28,15... | collective-permute-start | bytes 294920 | tf_op jit(solution)/shard_map/ppermute | solution.py:480
  119.8 37.6 %collective-permute-start.11 = (bf16[24,16,128]{2,1,0:T(8,128)(2,1)}, bf16[24,16,128]{2,1,0:T(8,128)(2,1)S(1)}, u32[]{:S(2)}, u32[]{:S(2)}) collective-permute-start(bf16[24,16,128]{2,1,0:T(8,128)(2,1)} %get-tuple-element.55), channel_id=1, source_target_pairs={{0,160},{4,164},{8,168},{12,172},{16,176},{20,180},{24,184},{28,18... | collective-permute-start | bytes 294920 | tf_op jit(solution)/shard_map/ppermute | solution.py:480
  141.0 16.5 %collective-permute-start.12 = (bf16[24,16,128]{2,1,0:T(8,128)(2,1)}, bf16[24,16,128]{2,1,0:T(8,128)(2,1)S(1)}, u32[]{:S(2)}, u32[]{:S(2)}) collective-permute-start(bf16[24,16,128]{2,1,0:T(8,128)(2,1)} %get-tuple-element.56), channel_id=1, source_target_pairs={{0,192},{4,196},{8,200},{12,204},{16,208},{20,212},{24,216},{28,22... | collective-permute-start | bytes 294920 | tf_op jit(solution)/shard_map/ppermute | solution.py:480
  146.7 10.8 %collective-permute-start.13 = (bf16[24,16,128]{2,1,0:T(8,128)(2,1)}, bf16[24,16,128]{2,1,0:T(8,128)(2,1)S(1)}, u32[]{:S(2)}, u32[]{:S(2)}) collective-permute-start(bf16[24,16,128]{2,1,0:T(8,128)(2,1)} %get-tuple-element.57), channel_id=1, source_target_pairs={{0,224},{4,228},{8,232},{12,236},{16,240},{20,244},{24,248},{28,25... | collective-permute-start | bytes 294920 | tf_op jit(solution)/shard_map/ppermute | solution.py:480
  167.6 9.5 %collective-permute-start.20 = (bf16[24,16,128]{2,1,0:T(8,128)(2,1)}, bf16[24,16,128]{2,1,0:T(8,128)(2,1)S(1)}, u32[]{:S(2)}, u32[]{:S(2)}) collective-permute-start(bf16[24,16,128]{2,1,0:T(8,128)(2,1)} %get-tuple-element.62), channel_id=1, source_target_pairs={{0,16},{4,20},{8,24},{12,28},{16,0},{20,4},{24,8},{28,12},{32,48},... | collective-permute-start | bytes 294920 | tf_op jit(solution)/shard_map/ppermute | solution.py:474
  169.3 8.9 %collective-permute-start.21 = (bf16[24,16,128]{2,1,0:T(8,128)(2,1)}, bf16[24,16,128]{2,1,0:T(8,128)(2,1)}, u32[]{:S(2)}, u32[]{:S(2)}) collective-permute-start(bf16[24,16,128]{2,1,0:T(8,128)(2,1)} %get-tuple-element.63), channel_id=1, source_target_pairs={{0,20},{4,16},{8,28},{12,24},{16,4},{20,0},{24,12},{28,8},{32,52},... | collective-permute-start | bytes 294920 | tf_op jit(solution)/shard_map/ppermute | solution.py:474
  170.8 43.3 %collective-permute-start.31 = (bf16[48,48,128]{2,1,0:T(8,128)(2,1)S(1)}, bf16[48,48,128]{2,1,0:T(8,128)(2,1)S(1)}, u32[]{:S(2)}, u32[]{:S(2)}) collective-permute-start(bf16[48,48,128]{2,1,0:T(8,128)(2,1)S(1)} %copy-done.10), channel_id=1, source_target_pairs={{0,1},{1,2},{2,3},{3,0},{4,5},{5,6},{6,7},{7,4},{8,9},{9,10},{10,1... | collective-permute-start | bytes 1769480 | tf_op jit(solution)/shard_map/ppermute | solution.py:527
  172.2 43.7 %collective-permute-start.32 = (bf16[48,48,128]{2,1,0:T(8,128)(2,1)S(1)}, bf16[48,48,128]{2,1,0:T(8,128)(2,1)S(1)}, u32[]{:S(2)}, u32[]{:S(2)}) collective-permute-start(bf16[48,48,128]{2,1,0:T(8,128)(2,1)S(1)} %copy-done.10), channel_id=1, source_target_pairs={{0,2},{1,3},{2,0},{3,1},{4,6},{5,7},{6,4},{7,5},{8,10},{9,11},{10,... | collective-permute-start | bytes 1769480 | tf_op jit(solution)/shard_map/ppermute | solution.py:527
  173.0 44.8 %collective-permute-start.33 = (bf16[48,48,128]{2,1,0:T(8,128)(2,1)S(1)}, bf16[48,48,128]{2,1,0:T(8,128)(2,1)}, u32[]{:S(2)}, u32[]{:S(2)}) collective-permute-start(bf16[48,48,128]{2,1,0:T(8,128)(2,1)S(1)} %copy-done.10), channel_id=1, source_target_pairs={{0,3},{1,0},{2,1},{3,2},{4,7},{5,4},{6,5},{7,6},{8,11},{9,8},{10,9... | collective-permute-start | bytes 1769480 | tf_op jit(solution)/shard_map/ppermute | solution.py:527
  185.7 17.7 %collective-permute-start.34 = (bf16[48,16,128]{2,1,0:T(8,128)(2,1)}, bf16[48,16,128]{2,1,0:T(8,128)(2,1)S(1)}, u32[]{:S(2)}, u32[]{:S(2)}) collective-permute-start(bf16[48,16,128]{2,1,0:T(8,128)(2,1)} %get-tuple-element.66.refs_8_.rest_4_), channel_id=1, source_target_pairs={{0,1},{1,2},{2,3},{3,0},{4,5},{5,6},{6,7},{7,4},{8,9},{9,10},{10,1... | collective-permute-start | bytes 589832 | tf_op jit(solution)/shard_map/ppermute | solution.py:527
  192.7 7.4 %collective-permute-start.25 = (bf16[24,16,128]{2,1,0:T(8,128)(2,1)}, bf16[24,16,128]{2,1,0:T(8,128)(2,1)S(1)}, u32[]{:S(2)}, u32[]{:S(2)}) collective-permute-start(bf16[24,16,128]{2,1,0:T(8,128)(2,1)} %get-tuple-element.69), channel_id=1, source_target_pairs={{0,64},{4,68},{8,72},{12,76},{16,80},{20,84},{24,88},{28,92},{32,9... | collective-permute-start | bytes 294920 | tf_op jit(solution)/shard_map/ppermute | solution.py:480
  200.1 8.1 %collective-permute-start.35 = (bf16[48,16,128]{2,1,0:T(8,128)(2,1)}, bf16[48,16,128]{2,1,0:T(8,128)(2,1)S(1)}, u32[]{:S(2)}, u32[]{:S(2)}) collective-permute-start(bf16[48,16,128]{2,1,0:T(8,128)(2,1)} %get-tuple-element.66.refs_8_.rest_4_), channel_id=1, source_target_pairs={{0,2},{1,3},{2,0},{3,1},{4,6},{5,7},{6,4},{7,5},{8,10},{9,11},{10,... | collective-permute-start | bytes 589832 | tf_op jit(solution)/shard_map/ppermute | solution.py:527
  203.4 8.0 %collective-permute-start.36 = (bf16[48,16,128]{2,1,0:T(8,128)(2,1)}, bf16[48,16,128]{2,1,0:T(8,128)(2,1)S(1)}, u32[]{:S(2)}, u32[]{:S(2)}) collective-permute-start(bf16[48,16,128]{2,1,0:T(8,128)(2,1)} %get-tuple-element.66.refs_8_.rest_4_), channel_id=1, source_target_pairs={{0,3},{1,0},{2,1},{3,2},{4,7},{5,4},{6,5},{7,6},{8,11},{9,8},{10,9... | collective-permute-start | bytes 589832 | tf_op jit(solution)/shard_map/ppermute | solution.py:527
  208.2 22.8 %collective-permute-start.26 = (bf16[24,16,128]{2,1,0:T(8,128)(2,1)}, bf16[24,16,128]{2,1,0:T(8,128)(2,1)S(1)}, u32[]{:S(2)}, u32[]{:S(2)}) collective-permute-start(bf16[24,16,128]{2,1,0:T(8,128)(2,1)} %get-tuple-element.70), channel_id=1, source_target_pairs={{0,96},{4,100},{8,104},{12,108},{16,112},{20,116},{24,120},{28,124... | collective-permute-start | bytes 294920 | tf_op jit(solution)/shard_map/ppermute | solution.py:480
  211.4 19.7 %collective-permute-start.27 = (bf16[24,16,128]{2,1,0:T(8,128)(2,1)}, bf16[24,16,128]{2,1,0:T(8,128)(2,1)S(1)}, u32[]{:S(2)}, u32[]{:S(2)}) collective-permute-start(bf16[24,16,128]{2,1,0:T(8,128)(2,1)} %get-tuple-element.71), channel_id=1, source_target_pairs={{0,128},{4,132},{8,136},{12,140},{16,144},{20,148},{24,152},{28,15... | collective-permute-start | bytes 294920 | tf_op jit(solution)/shard_map/ppermute | solution.py:480
  214.1 17.0 %collective-permute-start.28 = (bf16[24,16,128]{2,1,0:T(8,128)(2,1)}, bf16[24,16,128]{2,1,0:T(8,128)(2,1)S(1)}, u32[]{:S(2)}, u32[]{:S(2)}) collective-permute-start(bf16[24,16,128]{2,1,0:T(8,128)(2,1)} %get-tuple-element.72), channel_id=1, source_target_pairs={{0,160},{4,164},{8,168},{12,172},{16,176},{20,180},{24,184},{28,18... | collective-permute-start | bytes 294920 | tf_op jit(solution)/shard_map/ppermute | solution.py:480
  215.9 15.2 %collective-permute-start.29 = (bf16[24,16,128]{2,1,0:T(8,128)(2,1)}, bf16[24,16,128]{2,1,0:T(8,128)(2,1)S(1)}, u32[]{:S(2)}, u32[]{:S(2)}) collective-permute-start(bf16[24,16,128]{2,1,0:T(8,128)(2,1)} %get-tuple-element.73), channel_id=1, source_target_pairs={{0,192},{4,196},{8,200},{12,204},{16,208},{20,212},{24,216},{28,22... | collective-permute-start | bytes 294920 | tf_op jit(solution)/shard_map/ppermute | solution.py:480
  217.7 13.4 %collective-permute-start.30 = (bf16[24,16,128]{2,1,0:T(8,128)(2,1)}, bf16[24,16,128]{2,1,0:T(8,128)(2,1)S(1)}, u32[]{:S(2)}, u32[]{:S(2)}) collective-permute-start(bf16[24,16,128]{2,1,0:T(8,128)(2,1)} %get-tuple-element.74), channel_id=1, source_target_pairs={{0,224},{4,228},{8,232},{12,236},{16,240},{20,244},{24,248},{28,25... | collective-permute-start | bytes 294920 | tf_op jit(solution)/shard_map/ppermute | solution.py:480
  (55 other events, 450.7 us)
